TPU v7x, 32 devices: a whole 2x2x4 slice. The times are simulated.
32 devices in a mesh: req: 8 (over z, y), kvh: 2 (over x), ffn: 2 (over core).
Axes of the slice: x: 2, y: 2, z: 4, core: 2. Of those that a mesh axis runs over, the one named last changes fastest.
Arguments:
- queries: bfloat16 [8, 64, 8192], P('req', None, 'kvh'), may hold values from -8 to 8
- tree_keys: bfloat16 [8, 64, 1024], P('req', None, 'kvh'), may hold values from -4.5 to 4.5
- tree_token_values: bfloat16 [8, 64, 1024], P('req', None, 'kvh'), may hold values from -6 to 6
- cache_keys: bfloat16 [8, 8, 8192, 128], P('req', 'kvh', 'ffn'), may hold values from -4.5 to 4.5
- cached_value_rows: bfloat16 [8, 8, 8192, 128], P('req', 'kvh', 'ffn'), may hold values from -6 to 6
- lengths: int32 [8], replicated, may hold values from 1 to 8192, 16384 in all
- parents: int32 [8, 64], P('req'), may hold values from 0 to 63, as said below
- residual: float32 [512, 8192], P(('req', 'ffn'), 'kvh'), may hold values from -6 to 6
- out_weight: bfloat16 [8192, 8192], P('kvh', ('req', 'ffn')), may hold values from -0.0625 to 0.0625
- norm_gain: float32 [8192], P('kvh'), may hold values from 0.25 to 1.75
- gate_weight: bfloat16 [8192, 28672], P('kvh', ('req', 'ffn')), may hold values from -0.0625 to 0.0625
- up_weight: bfloat16 [8192, 28672], P('kvh', ('req', 'ffn')), may hold values from -0.0625 to 0.0625
- down_weight: bfloat16 [28672, 8192], P(('req', 'ffn'), 'kvh'), may hold values from -0.03125 to 0.03125
Outputs:
- layer_output: float32 [512, 8192], P(('req', 'ffn'), 'kvh')
Inputs may be any that keep to these rules, and one draw needn't show every extreme that they name: parents[r, 0] = 0, and parents[r, i] < i for every node i > 0. The lengths of all requests sum to 16384, and the largest is exactly 8192.
All inputs are finite; a program needn't handle non-finite values.
Results may differ from a plain program's by a relative error of at most 0.003.
Values may be sent and summed in bfloat16 or wider, within the bound.
A program may use at most 128 MiB of HBM per device.

v0:
```python
import functools
import math

import jax
import jax.numpy as jnp
from jax import lax
from jax.experimental import pallas as pl
from jax.experimental.pallas import tpu as pltpu
from jax.sharding import PartitionSpec as P

MASKED = -1e30
EPSILON = 1e-05


def attend(len_ref, q_ref, tk_ref, tv_ref, k_ref, v_ref, par_ref, o_ref, ml_ref, acc, stat, *, chunk, factor):
    live = len_ref[0]
    tree_live = len_ref[1]
    nodes = q_ref.shape[0]
    size = k_ref.shape[-1]
    group = q_ref.shape[1] // size
    rows = nodes * group
    q = jnp.concatenate([q_ref[:, g * size : (g + 1) * size] for g in range(group)], axis=0)
    acc[...] = jnp.zeros_like(acc)
    stat[0:1, :] = jnp.full((1, rows), MASKED, jnp.float32)
    stat[1:2, :] = jnp.zeros((1, rows), jnp.float32)

    def scores_of(keys):
        return lax.dot_general(keys, q, (((1,), (1,)), ((), ())), preferred_element_type=jnp.float32)

    def absorb(scores, usable, values):
        if usable is not None:
            scores = jnp.where(usable, scores, MASKED)
        old = stat[0:1, :]
        top = jnp.maximum(old, jnp.max(scores, axis=0, keepdims=True))
        weights = jnp.exp2(scores * factor - top * factor)
        if usable is not None:
            weights = jnp.where(usable, weights, 0.0)
        shrink = jnp.exp2((old - top) * factor)
        stat[0:1, :] = top
        stat[1:2, :] = stat[1:2, :] * shrink + jnp.sum(weights, axis=0, keepdims=True)
        acc[...] = acc[...] * shrink + lax.dot_general(
            values, weights.astype(jnp.bfloat16), (((0,), (0,)), ((), ())), preferred_element_type=jnp.float32
        )

    full = live // chunk

    def visit(c, carry):
        at = pl.ds(pl.multiple_of(c * chunk, chunk), chunk)
        absorb(scores_of(k_ref[0, at, :]), None, v_ref[0, at, :])
        return carry

    lax.fori_loop(0, full, visit, 0)

    @pl.when(live > full * chunk)
    def _():
        at = pl.ds(pl.multiple_of(full * chunk, chunk), chunk)
        spot = full * chunk + lax.broadcasted_iota(jnp.int32, (chunk, rows), 0)
        absorb(scores_of(k_ref[0, at, :]), spot < live, v_ref[0, at, :])

    @pl.when(tree_live > 0)
    def _():
        up = lax.broadcasted_iota(jnp.int32, (nodes, nodes), 0)
        across = lax.broadcasted_iota(jnp.int32, (nodes, nodes), 1)
        link = jnp.where(up == par_ref[...], 1.0, 0.0) + jnp.where(up == across, 1.0, 0.0)
        reach = jnp.minimum(link, 1.0)
        for _ in range((nodes - 1).bit_length()):
            half = reach.astype(jnp.bfloat16)
            reach = jnp.minimum(jnp.dot(half, half, preferred_element_type=jnp.float32), 1.0)
        row = lax.broadcasted_iota(jnp.int32, (nodes, rows), 0)
        col = lax.broadcasted_iota(jnp.int32, (nodes, rows), 1)
        spread = jnp.where(lax.rem(col, nodes) == row, 1.0, 0.0).astype(jnp.bfloat16)
        mask = jnp.dot(reach.astype(jnp.bfloat16), spread, preferred_element_type=jnp.float32)
        absorb(scores_of(tk_ref[...]), mask > 0.5, tv_ref[...])

    total = stat[1:2, :]
    out = (acc[...] / jnp.where(total > 0.0, total, 1.0)).T.astype(jnp.bfloat16)
    for g in range(group):
        o_ref[:, g * size : (g + 1) * size] = out[g * nodes : (g + 1) * nodes, :]
    ml_ref[0] = jnp.concatenate([stat[0:1, :] * (size**-0.5), total], axis=0)


def attention_part(queries, tree_keys, tree_values, keys, values, lengths2, parents):
    heads, span, size = keys.shape
    nodes, width = queries.shape
    wide = width // heads
    rows = wide // size * nodes
    chunk = math.gcd(span, 1024)
    body = functools.partial(attend, chunk=chunk, factor=size**-0.5 * math.log2(math.e))
    return pl.pallas_call(
        body,
        out_shape=(
            jax.ShapeDtypeStruct((nodes, width), jnp.bfloat16),
            jax.ShapeDtypeStruct((heads, 2, rows), jnp.float32),
        ),
        grid_spec=pltpu.PrefetchScalarGridSpec(
            num_scalar_prefetch=1,
            grid=(heads,),
            in_specs=[
                pl.BlockSpec((nodes, wide), lambda h, n: (0, h)),
                pl.BlockSpec((nodes, size), lambda h, n: (0, h)),
                pl.BlockSpec((nodes, size), lambda h, n: (0, h)),
                pl.BlockSpec((1, span, size), lambda h, n: (h, 0, 0)),
                pl.BlockSpec((1, span, size), lambda h, n: (h, 0, 0)),
                pl.BlockSpec((1, nodes), lambda h, n: (0, 0)),
            ],
            out_specs=(
                pl.BlockSpec((nodes, wide), lambda h, n: (0, h)),
                pl.BlockSpec((1, 2, rows), lambda h, n: (h, 0, 0)),
            ),
            scratch_shapes=[
                pltpu.VMEM((size, rows), jnp.float32),
                pltpu.VMEM((8, rows), jnp.float32),
            ],
        ),
        compiler_params=pltpu.CompilerParams(dimension_semantics=("arbitrary",)),
    )(lengths2, queries, tree_keys, tree_values, keys, values, parents)


MESH = pl.DeviceIdType.MESH
VMEM_LIMIT = 60 * 1024 * 1024


def split_count(n):
    lo = math.isqrt(n)
    while n % lo:
        lo -= 1
    return n // lo, lo


def ring_peers(n, me):
    return [lax.rem(me + d, n) for d in range(1, n)]


def staged_places(hi_n, lo_n, core_n):
    req = lax.axis_index("req")
    hi, lo, core = req // lo_n, lax.rem(req, lo_n), lax.axis_index("ffn")
    hi_peers = [(h, {"req": h * lo_n + lo}) for h in ring_peers(hi_n, hi)]
    lo_peers = [(b, {"req": hi * lo_n + b}) for b in ring_peers(lo_n, lo)]
    core_peers = [(c, {"ffn": c}) for c in ring_peers(core_n, core)]
    return hi, lo, core, hi_peers, lo_peers, core_peers


def meet(peers):
    barrier = pltpu.get_barrier_semaphore()
    for _, where in peers:
        pl.semaphore_signal(barrier, inc=1, device_id=where, device_id_type=MESH)
    pl.semaphore_wait(barrier, len(peers))


def remote(src, dst, send, recv, where):
    return pltpu.make_async_remote_copy(
        src_ref=src, dst_ref=dst, send_sem=send, recv_sem=recv, device_id=where, device_id_type=MESH
    )


def gather_body(x_ref, out_ref, send, recv, own_sem, *, dims, pieces):
    hi_n, lo_n, core_n = dims
    hi, lo, core, hi_peers, lo_peers, core_peers = staged_places(*dims)
    wide = x_ref.shape[1] // pieces
    meet(hi_peers + lo_peers + core_peers)
    own = pltpu.make_async_copy(x_ref, out_ref.at[hi, lo, core], own_sem)
    own.start()
    first, second, third = [], [], []
    for p in range(pieces):
        cols = pl.ds(p * wide, wide)
        group = []
        for d, (_, where) in enumerate(hi_peers):
            copy = remote(
                x_ref.at[:, cols], out_ref.at[hi, lo, core, :, cols], send.at[p, d], recv.at[p, d], where
            )
            copy.start()
            group.append(copy)
        first.append(group)
    own.wait()
    base = len(hi_peers)
    for step in range(pieces + 1):
        if step < pieces:
            cols = pl.ds(step * wide, wide)
            for copy in first[step]:
                copy.wait_recv()
            group = []
            for d, (_, where) in enumerate(lo_peers):
                part = out_ref.at[:, lo, core, :, cols]
                copy = remote(part, part, send.at[step, base + d], recv.at[step, base + d], where)
                copy.start()
                group.append(copy)
            second.append(group)
        if step > 0:
            p = step - 1
            cols = pl.ds(p * wide, wide)
            for copy in second[p]:
                copy.wait_recv()
            group = []
            for d, (_, where) in enumerate(core_peers):
                at = base + len(lo_peers) + d
                part = out_ref.at[:, :, core, :, cols]
                copy = remote(part, part, send.at[p, at], recv.at[p, at], where)
                copy.start()
                group.append(copy)
            third.append(group)
    for group in third:
        for copy in group:
            copy.wait_recv()
    for group in first + second + third:
        for copy in group:
            copy.wait_send()


def gather_tokens(x, collective_id):
    dims = (*split_count(lax.axis_size("req")), lax.axis_size("ffn"))
    rows, width = x.shape
    pieces = math.gcd(width // 128, 4)
    links = sum(dims) - 3
    vmem = pl.BlockSpec(memory_space=pltpu.VMEM)
    out = pl.pallas_call(
        functools.partial(gather_body, dims=dims, pieces=pieces),
        out_shape=jax.ShapeDtypeStruct((*dims, rows, width), x.dtype),
        in_specs=[vmem],
        out_specs=vmem,
        scratch_shapes=[
            pltpu.SemaphoreType.DMA((pieces, links)),
            pltpu.SemaphoreType.DMA((pieces, links)),
            pltpu.SemaphoreType.DMA,
        ],
        compiler_params=pltpu.CompilerParams(
            collective_id=collective_id, has_side_effects=True, vmem_limit_bytes=VMEM_LIMIT
        ),
    )(x)
    return out.reshape(math.prod(dims) * rows, width)


def scatter_body(x_ref, state_ref, out_ref, got_core, mid, own_mid, got_lo, low, own_low, got_hi, send, recv, *, dims, pieces):
    hi, lo, core, hi_peers, lo_peers, core_peers = staged_places(*dims)
    hi_n, lo_n, core_n = dims
    wide = x_ref.shape[-1] // pieces
    meet(hi_peers + lo_peers + core_peers)
    first, second, third = [], [], []
    for p in range(pieces):
        cols = pl.ds(p * wide, wide)
        group = []
        for d, (c, where) in enumerate(core_peers):
            copy = remote(
                x_ref.at[:, :, c, :, cols], got_core.at[d, :, :, :, cols], send.at[p, d], recv.at[p, d], where
            )
            copy.start()
            group.append(copy)
        first.append(group)
    base_lo = len(core_peers)
    base_hi = base_lo + len(lo_peers)
    for step in range(pieces + 2):
        if step < pieces:
            p = step
            cols = pl.ds(p * wide, wide)
            for copy in first[p]:
                copy.wait_recv()

            def add_core(h, carry):
                for b in range(lo_n):
                    total = x_ref[h, b, core, :, cols]
                    for d in range(core_n - 1):
                        total = total + got_core[d, h, b, :, cols]
                    mid[h, b, :, cols] = total.astype(jnp.bfloat16)
                    own_mid[h, b, :, cols] = total
                return carry

            lax.fori_loop(0, hi_n, add_core, 0)
            group = []
            for d, (b, where) in enumerate(lo_peers):
                at = base_lo + d
                copy = remote(mid.at[:, b, :, cols], got_lo.at[d, :, :, cols], send.at[p, at], recv.at[p, at], where)
                copy.start()
                group.append(copy)
            second.append(group)
        if 1 <= step <= pieces:
            p = step - 1
            cols = pl.ds(p * wide, wide)
            for copy in second[p]:
                copy.wait_recv()

            def add_lo(h, carry):
                total = own_mid[h, lo, :, cols]
                for d in range(lo_n - 1):
                    total = total + got_lo[d, h, :, cols].astype(jnp.float32)
                low[h, :, cols] = total.astype(jnp.bfloat16)
                own_low[h, :, cols] = total
                return carry

            lax.fori_loop(0, hi_n, add_lo, 0)
            group = []
            for d, (h, where) in enumerate(hi_peers):
                at = base_hi + d
                copy = remote(low.at[h, :, cols], got_hi.at[d, :, cols], send.at[p, at], recv.at[p, at], where)
                copy.start()
                group.append(copy)
            third.append(group)
        if step >= 2:
            p = step - 2
            cols = pl.ds(p * wide, wide)
            for copy in third[p]:
                copy.wait_recv()
            total = own_low[hi, :, cols]
            for d in range(hi_n - 1):
                total = total + got_hi[d, :, cols].astype(jnp.float32)
            out_ref[:, cols] = state_ref[:, cols] + total
    for group in first + second + third:
        for copy in group:
            copy.wait_send()


def scatter_tokens(x, state, collective_id):
    dims = (*split_count(lax.axis_size("req")), lax.axis_size("ffn"))
    hi_n, lo_n, core_n = dims
    rows, width = state.shape
    pieces = math.gcd(width // 128, 4)
    links = sum(dims) - 3
    vmem = pl.BlockSpec(memory_space=pltpu.VMEM)
    return pl.pallas_call(
        functools.partial(scatter_body, dims=dims, pieces=pieces),
        out_shape=jax.ShapeDtypeStruct(state.shape, jnp.float32),
        in_specs=[vmem, vmem],
        out_specs=vmem,
        scratch_shapes=[
            pltpu.VMEM((core_n - 1, hi_n, lo_n, rows, width), jnp.float32),
            pltpu.VMEM((hi_n, lo_n, rows, width), jnp.bfloat16),
            pltpu.VMEM((hi_n, lo_n, rows, width), jnp.float32),
            pltpu.VMEM((lo_n - 1, hi_n, rows, width), jnp.bfloat16),
            pltpu.VMEM((hi_n, rows, width), jnp.bfloat16),
            pltpu.VMEM((hi_n, rows, width), jnp.float32),
            pltpu.VMEM((hi_n - 1, rows, width), jnp.bfloat16),
            pltpu.SemaphoreType.DMA((pieces, links)),
            pltpu.SemaphoreType.DMA((pieces, links)),
        ],
        compiler_params=pltpu.CompilerParams(
            collective_id=collective_id, has_side_effects=True, vmem_limit_bytes=VMEM_LIMIT
        ),
    )(x.reshape(*dims, rows, width), state)


def gated_body(gate_ref, up_ref, own_gate_ref, own_up_ref, out_ref, got_gate, got_up, send, recv, *, pieces):
    n = gate_ref.shape[0]
    rows = gate_ref.shape[1]
    me = lax.axis_index("kvh")
    peers = [(k, {"kvh": k}) for k in ring_peers(n, me)]
    wide = gate_ref.shape[2] // pieces
    meet(peers)
    first, second = [], []
    for p in range(pieces):
        cols = pl.ds(p * wide, wide)
        group = []
        for d, (k, where) in enumerate(peers):
            for half, (src, dst) in enumerate(((gate_ref, got_gate), (up_ref, got_up))):
                copy = remote(
                    src.at[k, :, cols], dst.at[d, :, cols], send.at[half, p, d], recv.at[half, p, d], where
                )
                copy.start()
                group.append(copy)
        first.append(group)
    for p in range(pieces):
        cols = pl.ds(p * wide, wide)
        for copy in first[p]:
            copy.wait_recv()
        step = math.gcd(rows, 64)

        def activate(r, carry):
            at = pl.ds(pl.multiple_of(r * step, step), step)
            gate = own_gate_ref[at, cols]
            up = own_up_ref[at, cols]
            for d in range(n - 1):
                gate = gate + got_gate[d, at, cols].astype(jnp.float32)
                up = up + got_up[d, at, cols].astype(jnp.float32)
            out_ref[me, at, cols] = (gate / (1.0 + jnp.exp(-gate)) * up).astype(jnp.bfloat16)
            return carry

        lax.fori_loop(0, rows // step, activate, 0)
        group = []
        for d, (_, where) in enumerate(peers):
            part = out_ref.at[me, :, cols]
            copy = remote(part, part, send.at[2, p, d], recv.at[2, p, d], where)
            copy.start()
            group.append(copy)
        second.append(group)
    for group in second:
        for copy in group:
            copy.wait_recv()
    for group in first + second:
        for copy in group:
            copy.wait_send()


def gated(gate, up, collective_id):
    n = lax.axis_size("kvh")
    tokens, width = gate.shape
    rows = tokens // n
    pieces = math.gcd(width // 128, 7)
    gate, up = gate.reshape(n, rows, width), up.reshape(n, rows, width)
    me = lax.axis_index("kvh")
    own_gate = lax.dynamic_index_in_dim(gate, me, keepdims=False)
    own_up = lax.dynamic_index_in_dim(up, me, keepdims=False)
    vmem = pl.BlockSpec(memory_space=pltpu.VMEM)
    out = pl.pallas_call(
        functools.partial(gated_body, pieces=pieces),
        out_shape=jax.ShapeDtypeStruct((n, rows, width), jnp.bfloat16),
        in_specs=[vmem] * 4,
        out_specs=vmem,
        scratch_shapes=[
            pltpu.VMEM((n - 1, rows, width), jnp.bfloat16),
            pltpu.VMEM((n - 1, rows, width), jnp.bfloat16),
            pltpu.SemaphoreType.DMA((3, pieces, n - 1)),
            pltpu.SemaphoreType.DMA((3, pieces, n - 1)),
        ],
        compiler_params=pltpu.CompilerParams(
            collective_id=collective_id, has_side_effects=True, vmem_limit_bytes=VMEM_LIMIT
        ),
    )(gate.astype(jnp.bfloat16), up.astype(jnp.bfloat16), own_gate, own_up)
    return out.reshape(tokens, width)


def local(
    queries,
    tree_keys,
    tree_token_values,
    cache_keys,
    cached_value_rows,
    lengths,
    parents,
    residual,
    out_weight,
    norm_gain,
    gate_weight,
    up_weight,
    down_weight,
):
    heads, half_len, size = cache_keys.shape[1:]
    nodes = queries.shape[1]
    group = queries.shape[2] // (heads * size)
    request_index = lax.axis_index("req")
    half_index = lax.axis_index("ffn")
    halves = lax.axis_size("ffn")
    features = norm_gain.shape[0] * lax.axis_size("kvh")
    length = lax.dynamic_index_in_dim(lengths, request_index, keepdims=False)
    live_len = jnp.clip(length - half_index * half_len, 0, half_len)
    lengths2 = jnp.stack([live_len, (half_index == 0).astype(jnp.int32)])
    own, ml = attention_part(
        queries[0], tree_keys[0], tree_token_values[0], cache_keys[0], cached_value_rows[0], lengths2, parents
    )
    mine_rows = nodes // halves
    pair = lax.all_to_all(own, "ffn", split_axis=0, concat_axis=0, tiled=True).reshape(halves, mine_rows, -1)
    ml_pair = lax.all_gather(ml, "ffn")
    weights = ml_pair[:, :, 1] * jnp.exp(ml_pair[:, :, 0] - jnp.max(ml_pair[:, :, 0], axis=0))
    share = (weights / jnp.sum(weights, axis=0)).reshape(halves, heads * group, nodes)
    share = lax.dynamic_slice_in_dim(share, half_index * mine_rows, mine_rows, 2).transpose(0, 2, 1)[..., None]
    mixed = jnp.sum(pair.astype(jnp.float32).reshape(halves, mine_rows, heads * group, size) * share, axis=0)
    attention = mixed.astype(jnp.bfloat16).reshape(mine_rows, heads * group * size)
    partial_rows = jnp.dot(gather_tokens(attention, 1), out_weight, preferred_element_type=jnp.float32)
    regrouped = lax.all_to_all(
        partial_rows.astype(jnp.bfloat16), ("req", "ffn"), split_axis=0, concat_axis=1, tiled=True
    )
    shares = lax.all_to_all(regrouped, "kvh", split_axis=1, concat_axis=0, tiled=True)
    projected = jnp.sum(shares.astype(jnp.float32).reshape(-1, *residual.shape), axis=0)
    state = residual + projected
    squares = lax.psum(jnp.sum(state * state, axis=1), "kvh")
    normed = (state * lax.rsqrt(squares / features + EPSILON)[:, None] * norm_gain).astype(jnp.bfloat16)
    block_rows = gather_tokens(normed, 2)
    gate_part = jnp.dot(block_rows, gate_weight, preferred_element_type=jnp.float32)
    up_part = jnp.dot(block_rows, up_weight, preferred_element_type=jnp.float32)
    activation = gated(gate_part, up_part, 3)
    down_part = jnp.dot(activation, down_weight, preferred_element_type=jnp.float32)
    return scatter_tokens(down_part, state, 4)


def solution(mesh):
    in_specs = (
        P("req", None, "kvh"),
        P("req", None, "kvh"),
        P("req", None, "kvh"),
        P("req", "kvh", "ffn", None),
        P("req", "kvh", "ffn", None),
        P(),
        P("req", None),
        P(("req", "ffn"), "kvh"),
        P("kvh", ("req", "ffn")),
        P("kvh"),
        P("kvh", ("req", "ffn")),
        P("kvh", ("req", "ffn")),
        P(("req", "ffn"), "kvh"),
    )
    out_specs = P(("req", "ffn"), "kvh")
    return jax.shard_map(local, mesh=mesh, in_specs=in_specs, out_specs=out_specs, check_vma=False)
```

profile of v0, /device:TPU:1, one launch (start us, length us, event | category | flops | bytes accessed | tf_op | source)
XLA Modules:
  0.0 315.6 jit_solution(10149874736756071022)
XLA Ops:
  0.0 1.2 dynamic_slice.14
  1.9 0.6 pad_add_fusion.len_ref
  2.5 5.9 %shard_map.127 = (bf16[64,4096]{1,0:T(8,128)(2,1)}, f32[4,2,512]{2,1,0:T(2,128)}) custom-call(s32[2]{0:T(128)} %pad_add_fusion.len_ref, bf16[64,4096]{1,0:T(8,128)(2,1)} %bitcast.62, bf16[64,512]{1,0:T(8,128)(2,1)} %bitcast.66, bf16[64,512]{1,0:T(8,128)(2,1)} %bitcast.67, bf16[4,4096,128]{2,1,0:T(8,128)(2,1)} %bitcast.55, bf16[4,4096,128]{2,1,0:T(8,128)(2,1)} %bitcast.56, ...), custom_call_target="tpu_custom_call" | custom-call | tf_op jit(solution)/shard_map/pallas_call | solution.py:89
  8.3 18.9 %all-to-all-start = ((bf16[2,32,4096]{2,1,0:T(8,128)(2,1)}), bf16[2,32,4096]{2,1,0:T(8,128)(2,1)S(1)}, u32[]{:S(2)}, u32[]{:S(2)}) async-start(bf16[2,32,4096]{2,1,0:T(8,128)(2,1)} %bitcast.63), calls=%async_computation | async-start | bytes 1048576 | tf_op jit(solution)/shard_map/all_to_all | solution.py:447
  27.3 2.0 all-gather
  29.3 0.1 slice_reduce_fusion
  29.6 0.1 squeeze.43
  29.7 0.1 squeeze.44
  29.8 0.1 fusion.7
  30.0 0.3 mul.46
  30.3 0.2 mul.47
  30.5 0.8 multiply_reduce_fusion.x_ref
  31.4 40.3 %shard_map.128 = bf16[4,2,2,32,4096]{4,3,2,1,0:T(8,128)(2,1)} custom-call(bf16[32,4096]{1,0:T(8,128)(2,1)} %multiply_reduce_fusion.x_ref), custom_call_target="tpu_custom_call" | custom-call | tf_op jit(solution)/shard_map/pallas_call | solution.py:215
  71.7 5.8 %convolution_convert_fusion = bf16[512,512]{1,0:T(8,128)(2,1)S(1)} fusion(bf16[512,4096]{1,0:T(8,128)(2,1)} %bitcast.59, bf16[4096,512]{1,0:T(8,128)(2,1)} %param.21), kind=kOutput, calls=%fused_computation.8 | convolution fusion | flops 2147745792 | bytes 8912896 | tf_op jit(solution)/shard_map/dot_general | solution.py:454
  77.5 24.8 %all_to_all.38 = bf16[16,32,512]{2,1,0:T(8,128)(2,1)S(1)} all-to-all(bf16[16,32,512]{2,1,0:T(8,128)(2,1)S(1)} %bitcast.64), channel_id=1, replica_groups=mesh['req'=8,'kvh'=2,'ffn'=2] {'req','ffn'}, dimensions={0} | all-to-all | bytes 1048576 | tf_op jit(solution)/shard_map/all_to_all | solution.py:455
  102.3 0.3 copy.21
  102.6 0.4 all_to_all.33
  102.9 1.1 copy.22
  104.0 3.5 %all-to-all-start.2 = ((bf16[32,2,4096]{2,0,1:T(8,128)(2,1)}), bf16[32,2,4096]{2,0,1:T(8,128)(2,1)S(1)}, u32[]{:S(2)}, u32[]{:S(2)}) async-start(bf16[32,2,4096]{2,0,1:T(8,128)(2,1)} %copy.22), calls=%async_computation.2 | async-start | bytes 1048576 | tf_op jit(solution)/shard_map/all_to_all | solution.py:458
  107.5 7.7 %all-to-all-done.2 = bf16[32,2,4096]{2,0,1:T(8,128)(2,1)S(1)} async-done(((bf16[32,2,4096]{2,0,1:T(8,128)(2,1)}), bf16[32,2,4096]{2,0,1:T(8,128)(2,1)S(1)}, u32[]{:S(2)}, u32[]{:S(2)}) %all-to-all-start.2) | async-done | bytes 524320 | tf_op jit(solution)/shard_map/all_to_all | solution.py:458
  115.3 0.2 multiply_reduce_fusion.1
  115.5 4.0 %psum.7 = f32[32]{0:T(128)S(1)} all-reduce(f32[32]{0:T(128)S(1)} %get-tuple-element.11), channel_id=1, replica_groups=mesh['req'=8,'kvh'=2,'ffn'=2] {'kvh'}, use_global_device_ids=true, to_apply=%region_5.6 | all-reduce | flops 32 | bytes 256 | tf_op jit(solution)/shard_map/psum | solution.py:461
  119.5 0.8 multiply_convert_fusion.x_ref
  120.3 41.2 %shard_map.129 = bf16[4,2,2,32,4096]{4,3,2,1,0:T(8,128)(2,1)} custom-call(bf16[32,4096]{1,0:T(8,128)(2,1)} %multiply_convert_fusion.x_ref), custom_call_target="tpu_custom_call" | custom-call | tf_op jit(solution)/shard_map/pallas_call | solution.py:215
  161.5 14.5 %fusion.13 = (bf16[2,256,1792]{2,1,0:T(8,128)(2,1)}, f32[2,256,1792]{2,1,0:T(8,128)S(1)}) fusion(bf16[2,256,4096]{2,1,0:T(8,128)(2,1)} %bitcast.57, bf16[4096,1792]{1,0:T(8,128)(2,1)} %param.24), kind=kOutput, calls=%fused_computation.29 | convolution fusion | flops 7517110272 | bytes 24379392 | tf_op jit(solution)/shard_map/dot_general | solution.py:465
  176.0 12.5 %fusion.12 = (bf16[2,256,1792]{2,1,0:T(8,128)(2,1)}, f32[2,256,1792]{2,1,0:T(8,128)S(1)}) fusion(bf16[2,256,4096]{2,1,0:T(8,128)(2,1)S(1)} %bitcast.58, bf16[4096,1792]{1,0:T(8,128)(2,1)} %param.23), kind=kOutput, calls=%fused_computation.28 | convolution fusion | flops 7517110272 | bytes 24379392 | tf_op jit(solution)/shard_map/dot_general | solution.py:464
  188.5 1.3 dynamic-slice_bitcast_fusion.own_up_ref
  189.8 1.4 dynamic-slice_bitcast_fusion.1.own_gate_ref
  191.2 66.0 %shard_map.130 = bf16[2,256,1792]{2,1,0:T(8,128)(2,1)} custom-call(bf16[2,256,1792]{2,1,0:T(8,128)(2,1)} %get-tuple-element.15.gate_ref, bf16[2,256,1792]{2,1,0:T(8,128)(2,1)} %get-tuple-element.17.up_ref, f32[256,1792]{1,0:T(8,128)} %dynamic-slice_bitcast_fusion.1.own_gate_ref, f32[256,1792]{1,0:T(8,128)} %dynamic-slice_bitcast_fusion.own_up_ref), custom_call_target="tpu_custom_call" | custom-call | tf_op jit(solution)/shard_map/pallas_call | solution.py:400
  257.2 13.6 %fusion.x_ref = f32[4,2,2,32,4096]{4,3,2,1,0:T(8,128)} fusion(bf16[4,2,2,32,1792]{4,3,2,1,0:T(8,128)(2,1)} %bitcast.61, bf16[1792,4096]{1,0:T(8,128)(2,1)} %param.25), kind=kOutput, calls=%fused_computation | convolution fusion | flops 7516192768 | bytes 24903680 | tf_op jit(solution)/shard_map/dot_general | solution.py:467
  270.7 43.0 %shard_map.131 = f32[32,4096]{1,0:T(8,128)} custom-call(f32[4,2,2,32,4096]{4,3,2,1,0:T(8,128)} %fusion.x_ref, f32[32,4096]{1,0:T(8,128)} %copy-done), custom_call_target="tpu_custom_call" | custom-call | tf_op jit(solution)/shard_map/pallas_call | solution.py:317
  313.8 1.9 copy.29
  (17 shorter events, 0.4 us)
Async XLA Ops:
  8.3 22.2 %all-to-all-start = ((bf16[2,32,4096]{2,1,0:T(8,128)(2,1)}), bf16[2,32,4096]{2,1,0:T(8,128)(2,1)S(1)}, u32[]{:S(2)}, u32[]{:S(2)}) async-start(bf16[2,32,4096]{2,1,0:T(8,128)(2,1)} %bitcast.63), calls=%async_computation | async-start | bytes 1048576 | tf_op jit(solution)/shard_map/all_to_all | solution.py:447
  77.5 37.9 %copy-start.2 = (f32[32,4096]{1,0:T(8,128)S(1)}, f32[32,4096]{1,0:T(8,128)}, u32[]{:S(2)}) copy-start(f32[32,4096]{1,0:T(8,128)} %param.20) | copy-start | bytes 1572868
  77.5 42.0 %copy-start.3 = (f32[4096]{0:T(1024)S(1)}, f32[4096]{0:T(1024)}, u32[]{:S(2)}) copy-start(f32[4096]{0:T(1024)} %param.22) | copy-start | bytes 49156
  104.0 11.2 %all-to-all-start.2 = ((bf16[32,2,4096]{2,0,1:T(8,128)(2,1)}), bf16[32,2,4096]{2,0,1:T(8,128)(2,1)S(1)}, u32[]{:S(2)}, u32[]{:S(2)}) async-start(bf16[32,2,4096]{2,0,1:T(8,128)(2,1)} %copy.22), calls=%async_computation.2 | async-start | bytes 1048576 | tf_op jit(solution)/shard_map/all_to_all | solution.py:458
  115.5 60.5 %copy-start = (f32[32,4096]{1,0:T(8,128)}, f32[32,4096]{1,0:T(8,128)S(1)}, u32[]{:S(2)}) copy-start(f32[32,4096]{1,0:T(8,128)S(1)} %get-tuple-element.12.state_ref) | copy-start | bytes 1572868
  161.5 14.5 %copy-start.1 = (bf16[4,2,2,32,4096]{4,3,2,1,0:T(8,128)(2,1)S(1)}, bf16[4,2,2,32,4096]{4,3,2,1,0:T(8,128)(2,1)}, u32[]{:S(2)}) copy-start(bf16[4,2,2,32,4096]{4,3,2,1,0:T(8,128)(2,1)} %shard_map.129) | copy-start | bytes 12582916
where the time goes:
time: 318 us; the launch traced here: 316 us
  Pallas kernels  196 us (62%)
  matrix products  46.3 us (15%)
  blocking collectives  30.8 us (10%)
  starting transfers between devices  22.4 us (7%)
  local copies, waits for them, and re-layouts  8.6 us (3%)
  waiting for transfers between devices  7.69 us (2%)
    pallas_call x2, Pallas kernels, gather_tokens(): pl.pallas_call(functools.partial(gather_body, dims=dims, pieces=pieces),...  81.5 us
    pallas_call x1, Pallas kernels, gated(): pl.pallas_call(functools.partial(gated_body, pieces=pieces), out_shape=ja...  66 us
    pallas_call x1, Pallas kernels, scatter_tokens(): pl.pallas_call(functools.partial(scatter_body, dims=dims, pieces=pieces),...  43 us
    all_to_all x1, blocking collectives, local(): lax.all_to_all(partial_rows.astype(jnp.bfloat16), ('req', 'ffn'), split_a...  24.8 us
    all_to_all x1, starting transfers between devices, local(): lax.all_to_all(own, 'ffn', split_axis=0, concat_axis=0, tiled=True)  18.9 us
    dot_general x1, matrix products, local(): up_part = jnp.dot(block_rows, up_weight, preferred_element_type=jnp.float32)  14.5 us
    dot_general x1, matrix products, local(): jnp.dot(activation, down_weight, preferred_element_type=jnp.float32)  13.6 us
    dot_general x1, matrix products, local(): jnp.dot(block_rows, gate_weight, preferred_element_type=jnp.float32)  12.5 us
  transfers between devices with their start and end apart: 2, of which 1 were waited for; matrix products, arithmetic and copies ran while one was open for 0% of the time, Pallas kernels for 0%

commit v1 on v0

--- a/solution.py
+++ b/solution.py
@@ -229,190 +229,393 @@
     return out.reshape(math.prod(dims) * rows, width)
 
 
-def scatter_body(x_ref, state_ref, out_ref, got_core, mid, own_mid, got_lo, low, own_low, got_hi, send, recv, *, dims, pieces):
-    hi, lo, core, hi_peers, lo_peers, core_peers = staged_places(*dims)
-    hi_n, lo_n, core_n = dims
-    wide = x_ref.shape[-1] // pieces
-    meet(hi_peers + lo_peers + core_peers)
-    first, second, third = [], [], []
-    for p in range(pieces):
-        cols = pl.ds(p * wide, wide)
-        group = []
-        for d, (c, where) in enumerate(core_peers):
-            copy = remote(
-                x_ref.at[:, :, c, :, cols], got_core.at[d, :, :, :, cols], send.at[p, d], recv.at[p, d], where
-            )
+def lane_block(width, most):
+    return max(b for b in range(128, most + 1, 128) if width % b == 0)
+
+
+def ffn_body(
+    x_ref, state_ref, gate_hbm, up_hbm, down_hbm, out_ref,
+    gath, wgu, wd, rbuf, part, got, act, dbuf, got_core, mid, own_mid, got_lo, low, own_low, got_hi,
+    own_sem, w_sem, wd_sem, g_send, g_recv, p_send, p_recv, a_send, a_recv, c_send, c_recv, l_send, l_recv, h_send, h_recv,
+    *, dims, kn, rc,
+):
+    hn, ln, cn = dims
+    hi, lo, core, _, _, _ = staged_places(*dims)
+    k = lax.axis_index("kvh")
+    chunks = x_ref.shape[0] // rc
+    blocks = hn * ln
+    hc = wgu.shape[2] // 2
+    hs = wgu.shape[0]
+    total_rows = blocks * cn * rc
+    keep = total_rows // kn
+    fw = wd.shape[2]
+    fs = x_ref.shape[1] // fw
+    wd_slots, d_slots, r_slots, m_slots = wd.shape[0], dbuf.shape[0], rbuf.shape[0], own_mid.shape[0]
+    to_hi = lambda d: (lax.rem(hi + d, hn), {"req": lax.rem(hi + d, hn) * ln + lo})
+    to_lo = lambda d: (lax.rem(lo + d, ln), {"req": hi * ln + lax.rem(lo + d, ln)})
+    to_core = lambda d: (lax.rem(core + d, cn), {"ffn": lax.rem(core + d, cn)})
+    to_kvh = lambda d: (lax.rem(k + d, kn), {"kvh": lax.rem(k + d, kn)})
+    meet(
+        [to_hi(d) for d in range(1, hn)]
+        + [to_lo(d) for d in range(1, ln)]
+        + [to_core(d) for d in range(1, cn)]
+        + [to_kvh(d) for d in range(1, kn)]
+    )
+
+    def weight_copies(h):
+        cols = pl.ds(pl.multiple_of(h * hc, hc), hc)
+        return (
+            pltpu.make_async_copy(gate_hbm.at[:, cols], wgu.at[h, :, pl.ds(0, hc)], w_sem.at[0, h]),
+            pltpu.make_async_copy(up_hbm.at[:, cols], wgu.at[h, :, pl.ds(hc, hc)], w_sem.at[1, h]),
+        )
+
+    def down_copy(j):
+        slot = lax.rem(j, wd_slots)
+        cols = pl.ds(pl.multiple_of(lax.rem(j, fs) * fw, fw), fw)
+        return pltpu.make_async_copy(down_hbm.at[:, cols], wd.at[slot], wd_sem.at[slot])
+
+    def rows_of(h, b, c):
+        return pl.ds(pl.multiple_of(((c * ln + b) * hn + h) * rc, rc), rc)
+
+    def place(c, e, g, f):
+        return gath.at[c, rows_of(lax.rem(hi + hn - e, hn), lax.rem(lo + ln - g, ln), f), :]
+
+    base_lo = hn - 1
+    base_core = base_lo + hn * (ln - 1)
+
+    def hi_copy(c, d):
+        at = d - 1
+        src = x_ref.at[pl.ds(c * rc, rc), :]
+        return remote(src, place(c, 0, 0, core), g_send.at[c, at], g_recv.at[c, at], to_hi(d)[1])
+
+    def lo_copy(c, e, d):
+        at = base_lo + e * (ln - 1) + d - 1
+        src = x_ref.at[pl.ds(c * rc, rc), :] if e == 0 else place(c, e, 0, core)
+        return remote(src, place(c, e, 0, core), g_send.at[c, at], g_recv.at[c, at], to_lo(d)[1])
+
+    def core_copy(c, e, g, d):
+        at = base_core + (e * ln + g) * (cn - 1) + d - 1
+        src = x_ref.at[pl.ds(c * rc, rc), :] if e == 0 and g == 0 else place(c, e, g, core)
+        return remote(src, place(c, e, g, core), g_send.at[c, at], g_recv.at[c, at], to_core(d)[1])
+
+    hi_order = sorted(range(1, hn), key=lambda d: min(d, hn - d))
+
+    def own_copy(c):
+        return pltpu.make_async_copy(x_ref.at[pl.ds(c * rc, rc), :], place(c, 0, 0, core), own_sem.at[c])
+
+    def gather_start(c):
+        for d in hi_order:
+            hi_copy(c, d).start()
+        for d in range(1, ln):
+            lo_copy(c, 0, d).start()
+        for d in range(1, cn):
+            core_copy(c, 0, 0, d).start()
+        own_copy(c).start()
+
+    def gather_hi(c):
+        for e in hi_order:
+            hi_copy(c, e).wait_recv()
+            for d in range(1, ln):
+                lo_copy(c, e, d).start()
+            for d in range(1, cn):
+                core_copy(c, e, 0, d).start()
+
+    def gather_lo(c):
+        for e in [0] + hi_order:
+            for g in range(1, ln):
+                lo_copy(c, e, g).wait_recv()
+                for d in range(1, cn):
+                    core_copy(c, e, g, d).start()
+
+    def gather_end(c):
+        for e in [0] + hi_order:
+            for g in range(ln):
+                for d in range(1, cn):
+                    core_copy(c, e, g, d).wait_recv()
+        own_copy(c).wait()
+
+    def gather_sent(c):
+        for d in range(1, hn):
+            hi_copy(c, d).wait_send()
+        for e in range(hn):
+            for d in range(1, ln):
+                lo_copy(c, e, d).wait_send()
+            for g in range(ln):
+                for d in range(1, cn):
+                    core_copy(c, e, g, d).wait_send()
+
+    def part_copy(s, d):
+        return remote(part.at[s, d - 1], got.at[s, d - 1], p_send.at[s, d - 1], p_recv.at[s, d - 1], to_kvh(d)[1])
+
+    def hidden(c, h):
+        s = c * hs + h
+        slot = lax.rem(s, r_slots)
+        rbuf[slot] = jnp.dot(gath[c], wgu[h], preferred_element_type=jnp.float32)
+        for d in range(1, kn):
+            group = pl.ds(pl.multiple_of(to_kvh(d)[0] * keep, keep), keep)
+            part[s, d - 1] = rbuf[slot, group, :].astype(jnp.bfloat16)
+            part_copy(s, d).start()
+
+    mine = pl.ds(pl.multiple_of(k * keep, keep), keep)
+
+    def act_copy(s, d):
+        c, h = lax.div(s, hs), lax.rem(s, hs)
+        spot = act.at[c, mine, pl.ds(pl.multiple_of(h * hc, hc), hc)]
+        return remote(spot, spot, a_send.at[s, d - 1], a_recv.at[s, d - 1], to_kvh(d)[1])
+
+    def activate(s):
+        c, h = lax.div(s, hs), lax.rem(s, hs)
+        slot = lax.rem(s, r_slots)
+        for d in range(1, kn):
+            part_copy(s, d).wait_recv()
+        gate = rbuf[slot, mine, pl.ds(0, hc)]
+        up = rbuf[slot, mine, pl.ds(hc, hc)]
+        for d in range(kn - 1):
+            gate = gate + got[s, d, :, pl.ds(0, hc)].astype(jnp.float32)
+            up = up + got[s, d, :, pl.ds(hc, hc)].astype(jnp.float32)
+        act[c, mine, pl.ds(pl.multiple_of(h * hc, hc), hc)] = (gate / (1.0 + jnp.exp(-gate)) * up).astype(jnp.bfloat16)
+        for d in range(1, kn):
+            act_copy(s, d).start()
+
+    def activated(c):
+        def one(h, carry):
+            for d in range(1, kn):
+                act_copy(c * hs + h, d).wait_recv()
+            return carry
+
+        lax.fori_loop(0, hs, one, 0)
+
+    def down_send(j, d):
+        half = pl.ds(pl.multiple_of(to_core(d)[0] * (blocks * rc), blocks * rc), blocks * rc)
+        return remote(
+            dbuf.at[lax.rem(j, d_slots), half, :], got_core.at[j, d - 1], c_send.at[j, d - 1], c_recv.at[j, d - 1], to_core(d)[1]
+        )
+
+    def mid_send(j, d):
+        return remote(mid.at[j, d - 1], got_lo.at[j, d - 1], l_send.at[j, d - 1], l_recv.at[j, d - 1], to_lo(d)[1])
+
+    def low_send(j, d):
+        return remote(low.at[j, d - 1], got_hi.at[j, d - 1], h_send.at[j, d - 1], h_recv.at[j, d - 1], to_hi(d)[1])
+
+    def down(j):
+        c = lax.div(j, fs)
+        slot = lax.rem(j, d_slots)
+
+        @pl.when(j >= d_slots)
+        def _():
+            for d in range(1, cn):
+                down_send(j - d_slots, d).wait_send()
+
+        down_copy(j).wait()
+        dbuf[slot] = jnp.dot(act[c], wd[lax.rem(j, wd_slots)], preferred_element_type=jnp.float32)
+
+        @pl.when(j + wd_slots < chunks * fs)
+        def _():
+            down_copy(j + wd_slots).start()
+
+        for d in range(1, cn):
+            down_send(j, d).start()
+
+    def add_core(j):
+        slot = lax.rem(j, d_slots)
+        for d in range(1, cn):
+            down_send(j, d).wait_recv()
+
+        def total(b):
+            at = pl.multiple_of(b * (hn * rc), hn * rc)
+            here = pl.multiple_of(core * (blocks * rc), blocks * rc) + at
+            result = dbuf[slot, pl.ds(pl.multiple_of(here, hn * rc), hn * rc), :]
+            for d in range(cn - 1):
+                result = result + got_core[j, d, pl.ds(at, hn * rc), :]
+            return result
+
+        for d in range(1, ln):
+            mid[j, d - 1] = total(to_lo(d)[0]).astype(jnp.bfloat16)
+            mid_send(j, d).start()
+        own_mid[lax.rem(j, m_slots)] = total(lo)
+
+    def add_lo(j):
+        slot = lax.rem(j, m_slots)
+        for d in range(1, ln):
+            mid_send(j, d).wait_recv()
+
+        def total(h):
+            at = pl.ds(pl.multiple_of(h * rc, rc), rc)
+            result = own_mid[slot, at, :]
+            for d in range(ln - 1):
+                result = result + got_lo[j, d, at, :].astype(jnp.float32)
+            return result
+
+        for d in range(1, hn):
+            low[j, d - 1] = total(to_hi(d)[0]).astype(jnp.bfloat16)
+            low_send(j, d).start()
+        own_low[slot] = total(hi)
+
+    def add_hi(j):
+        c, n = lax.div(j, fs), lax.rem(j, fs)
+        for d in range(1, hn):
+            low_send(j, d).wait_recv()
+        result = own_low[lax.rem(j, m_slots)]
+        for d in range(hn - 1):
+            result = result + got_hi[j, d].astype(jnp.float32)
+        at = (pl.ds(pl.multiple_of(c * rc, rc), rc), pl.ds(pl.multiple_of(n * fw, fw), fw))
+        out_ref[at] = state_ref[at] + result
+
+    pieces = chunks * fs
+    lag = 2
+
+    def piece(j):
+        for depth, stage in enumerate((down, add_core, add_lo, add_hi)):
+
+            @pl.when((j >= depth * lag) & (j < pieces + depth * lag))
+            def _(depth=depth, stage=stage):
+                stage(j - depth * lag)
+
+    for h in range(hs):
+        for copy in weight_copies(h):
             copy.start()
-            group.append(copy)
-        first.append(group)
-    base_lo = len(core_peers)
-    base_hi = base_lo + len(lo_peers)
-    for step in range(pieces + 2):
-        if step < pieces:
-            p = step
-            cols = pl.ds(p * wide, wide)
-            for copy in first[p]:
-                copy.wait_recv()
-
-            def add_core(h, carry):
-                for b in range(lo_n):
-                    total = x_ref[h, b, core, :, cols]
-                    for d in range(core_n - 1):
-                        total = total + got_core[d, h, b, :, cols]
-                    mid[h, b, :, cols] = total.astype(jnp.bfloat16)
-                    own_mid[h, b, :, cols] = total
-                return carry
-
-            lax.fori_loop(0, hi_n, add_core, 0)
-            group = []
-            for d, (b, where) in enumerate(lo_peers):
-                at = base_lo + d
-                copy = remote(mid.at[:, b, :, cols], got_lo.at[d, :, :, cols], send.at[p, at], recv.at[p, at], where)
-                copy.start()
-                group.append(copy)
-            second.append(group)
-        if 1 <= step <= pieces:
-            p = step - 1
-            cols = pl.ds(p * wide, wide)
-            for copy in second[p]:
-                copy.wait_recv()
-
-            def add_lo(h, carry):
-                total = own_mid[h, lo, :, cols]
-                for d in range(lo_n - 1):
-                    total = total + got_lo[d, h, :, cols].astype(jnp.float32)
-                low[h, :, cols] = total.astype(jnp.bfloat16)
-                own_low[h, :, cols] = total
-                return carry
-
-            lax.fori_loop(0, hi_n, add_lo, 0)
-            group = []
-            for d, (h, where) in enumerate(hi_peers):
-                at = base_hi + d
-                copy = remote(low.at[h, :, cols], got_hi.at[d, :, cols], send.at[p, at], recv.at[p, at], where)
-                copy.start()
-                group.append(copy)
-            third.append(group)
-        if step >= 2:
-            p = step - 2
-            cols = pl.ds(p * wide, wide)
-            for copy in third[p]:
-                copy.wait_recv()
-            total = own_low[hi, :, cols]
-            for d in range(hi_n - 1):
-                total = total + got_hi[d, :, cols].astype(jnp.float32)
-            out_ref[:, cols] = state_ref[:, cols] + total
-    for group in first + second + third:
-        for copy in group:
-            copy.wait_send()
-
-
-def scatter_tokens(x, state, collective_id):
-    dims = (*split_count(lax.axis_size("req")), lax.axis_size("ffn"))
-    hi_n, lo_n, core_n = dims
-    rows, width = state.shape
-    pieces = math.gcd(width // 128, 4)
-    links = sum(dims) - 3
+    for j in range(min(wd_slots, pieces)):
+        down_copy(j).start()
+    gather_start(0)
+    gather_hi(0)
+    gather_lo(0)
+    for c in range(1, chunks):
+        gather_start(c)
+    gather_end(0)
+    behind = 2
+    marks = {3: gather_hi, 5: gather_lo, hs - 1: gather_end}
+    per = -(-fs // (hs - 3))
+    for c in range(chunks):
+
+        def step(h, carry, c=c):
+            if c == 0:
+                for copy in weight_copies(h):
+                    copy.wait()
+            hidden(c, h)
+
+            @pl.when(c * hs + h >= behind)
+            def _():
+                activate(c * hs + h - behind)
+
+            if c + 1 < chunks:
+                for at, stage in marks.items():
+
+                    @pl.when(h == at)
+                    def _(stage=stage):
+                        stage(c + 1)
+
+            if c > 0:
+
+                @pl.when(h == 3)
+                def _():
+                    activated(c - 1)
+
+                @pl.when(h >= 3)
+                def _():
+                    def one(i, carry):
+                        piece((c - 1) * fs + (h - 3) * per + i)
+                        return carry
+
+                    lax.fori_loop(0, jnp.minimum(per, fs - (h - 3) * per), one, 0)
+
+            return carry
+
+        lax.fori_loop(0, hs, step, 0)
+    for s in range(chunks * hs - behind, chunks * hs):
+        activate(s)
+    activated(chunks - 1)
+
+    def last(j, carry):
+        piece(j)
+        return carry
+
+    lax.fori_loop((chunks - 1) * fs, pieces + 3 * lag, last, 0)
+    for c in range(chunks):
+        gather_sent(c)
+
+    def sent_steps(s, carry):
+        for d in range(1, kn):
+            part_copy(s, d).wait_send()
+            act_copy(s, d).wait_send()
+        return carry
+
+    lax.fori_loop(0, chunks * hs, sent_steps, 0)
+
+    def sent_pieces(j, carry):
+        @pl.when(j >= pieces - d_slots)
+        def _():
+            for d in range(1, cn):
+                down_send(j, d).wait_send()
+
+        for d in range(1, ln):
+            mid_send(j, d).wait_send()
+        for d in range(1, hn):
+            low_send(j, d).wait_send()
+        return carry
+
+    lax.fori_loop(0, pieces, sent_pieces, 0)
+
+
+def feed_forward(x, state, gate_weight, up_weight, down_weight, collective_id):
+    hn, ln = split_count(lax.axis_size("req"))
+    cn, kn = lax.axis_size("ffn"), lax.axis_size("kvh")
+    rows, width = x.shape
+    rc = math.gcd(rows, 16)
+    chunks = rows // rc
+    hidden = gate_weight.shape[1]
+    hc = lane_block(hidden, 256)
+    hs = hidden // hc
+    fw = lane_block(width, max(128, width // 8))
+    pieces = chunks * (width // fw)
+    tokens = hn * ln * cn * rc
+    keep = tokens // kn
+    links = (hn - 1) + hn * (ln - 1) + hn * ln * (cn - 1)
     vmem = pl.BlockSpec(memory_space=pltpu.VMEM)
+    hbm = pl.BlockSpec(memory_space=pl.ANY)
+    f32, b16 = jnp.float32, jnp.bfloat16
+    dma = pltpu.SemaphoreType.DMA
+    steps = chunks * hs
     return pl.pallas_call(
-        functools.partial(scatter_body, dims=dims, pieces=pieces),
-        out_shape=jax.ShapeDtypeStruct(state.shape, jnp.float32),
-        in_specs=[vmem, vmem],
+        functools.partial(ffn_body, dims=(hn, ln, cn), kn=kn, rc=rc),
+        out_shape=jax.ShapeDtypeStruct(state.shape, f32),
+        in_specs=[vmem, vmem, hbm, hbm, hbm],
         out_specs=vmem,
         scratch_shapes=[
-            pltpu.VMEM((core_n - 1, hi_n, lo_n, rows, width), jnp.float32),
-            pltpu.VMEM((hi_n, lo_n, rows, width), jnp.bfloat16),
-            pltpu.VMEM((hi_n, lo_n, rows, width), jnp.float32),
-            pltpu.VMEM((lo_n - 1, hi_n, rows, width), jnp.bfloat16),
-            pltpu.VMEM((hi_n, rows, width), jnp.bfloat16),
-            pltpu.VMEM((hi_n, rows, width), jnp.float32),
-            pltpu.VMEM((hi_n - 1, rows, width), jnp.bfloat16),
-            pltpu.SemaphoreType.DMA((pieces, links)),
-            pltpu.SemaphoreType.DMA((pieces, links)),
+            pltpu.VMEM((chunks, tokens, width), b16),
+            pltpu.VMEM((hs, width, 2 * hc), b16),
+            pltpu.VMEM((3, hidden, fw), b16),
+            pltpu.VMEM((3, tokens, 2 * hc), f32),
+            pltpu.VMEM((steps, kn - 1, keep, 2 * hc), b16),
+            pltpu.VMEM((steps, kn - 1, keep, 2 * hc), b16),
+            pltpu.VMEM((chunks, tokens, hidden), b16),
+            pltpu.VMEM((4, tokens, fw), f32),
+            pltpu.VMEM((pieces, cn - 1, hn * ln * rc, fw), f32),
+            pltpu.VMEM((pieces, ln - 1, hn * rc, fw), b16),
+            pltpu.VMEM((4, hn * rc, fw), f32),
+            pltpu.VMEM((pieces, ln - 1, hn * rc, fw), b16),
+            pltpu.VMEM((pieces, hn - 1, rc, fw), b16),
+            pltpu.VMEM((4, rc, fw), f32),
+            pltpu.VMEM((pieces, hn - 1, rc, fw), b16),
+            dma((chunks,)),
+            dma((2, hs)),
+            dma((3,)),
+            dma((chunks, links)),
+            dma((chunks, links)),
+            dma((steps, kn - 1)),
+            dma((steps, kn - 1)),
+            dma((steps, kn - 1)),
+            dma((steps, kn - 1)),
+            dma((pieces, cn - 1)),
+            dma((pieces, cn - 1)),
+            dma((pieces, ln - 1)),
+            dma((pieces, ln - 1)),
+            dma((pieces, hn - 1)),
+            dma((pieces, hn - 1)),
         ],
         compiler_params=pltpu.CompilerParams(
-            collective_id=collective_id, has_side_effects=True, vmem_limit_bytes=VMEM_LIMIT
+            collective_id=collective_id, has_side_effects=True, vmem_limit_bytes=63 * 1024 * 1024
         ),
-    )(x.reshape(*dims, rows, width), state)
-
-
-def gated_body(gate_ref, up_ref, own_gate_ref, own_up_ref, out_ref, got_gate, got_up, send, recv, *, pieces):
-    n = gate_ref.shape[0]
-    rows = gate_ref.shape[1]
-    me = lax.axis_index("kvh")
-    peers = [(k, {"kvh": k}) for k in ring_peers(n, me)]
-    wide = gate_ref.shape[2] // pieces
-    meet(peers)
-    first, second = [], []
-    for p in range(pieces):
-        cols = pl.ds(p * wide, wide)
-        group = []
-        for d, (k, where) in enumerate(peers):
-            for half, (src, dst) in enumerate(((gate_ref, got_gate), (up_ref, got_up))):
-                copy = remote(
-                    src.at[k, :, cols], dst.at[d, :, cols], send.at[half, p, d], recv.at[half, p, d], where
-                )
-                copy.start()
-                group.append(copy)
-        first.append(group)
-    for p in range(pieces):
-        cols = pl.ds(p * wide, wide)
-        for copy in first[p]:
-            copy.wait_recv()
-        step = math.gcd(rows, 64)
-
-        def activate(r, carry):
-            at = pl.ds(pl.multiple_of(r * step, step), step)
-            gate = own_gate_ref[at, cols]
-            up = own_up_ref[at, cols]
-            for d in range(n - 1):
-                gate = gate + got_gate[d, at, cols].astype(jnp.float32)
-                up = up + got_up[d, at, cols].astype(jnp.float32)
-            out_ref[me, at, cols] = (gate / (1.0 + jnp.exp(-gate)) * up).astype(jnp.bfloat16)
-            return carry
-
-        lax.fori_loop(0, rows // step, activate, 0)
-        group = []
-        for d, (_, where) in enumerate(peers):
-            part = out_ref.at[me, :, cols]
-            copy = remote(part, part, send.at[2, p, d], recv.at[2, p, d], where)
-            copy.start()
-            group.append(copy)
-        second.append(group)
-    for group in second:
-        for copy in group:
-            copy.wait_recv()
-    for group in first + second:
-        for copy in group:
-            copy.wait_send()
-
-
-def gated(gate, up, collective_id):
-    n = lax.axis_size("kvh")
-    tokens, width = gate.shape
-    rows = tokens // n
-    pieces = math.gcd(width // 128, 7)
-    gate, up = gate.reshape(n, rows, width), up.reshape(n, rows, width)
-    me = lax.axis_index("kvh")
-    own_gate = lax.dynamic_index_in_dim(gate, me, keepdims=False)
-    own_up = lax.dynamic_index_in_dim(up, me, keepdims=False)
-    vmem = pl.BlockSpec(memory_space=pltpu.VMEM)
-    out = pl.pallas_call(
-        functools.partial(gated_body, pieces=pieces),
-        out_shape=jax.ShapeDtypeStruct((n, rows, width), jnp.bfloat16),
-        in_specs=[vmem] * 4,
-        out_specs=vmem,
-        scratch_shapes=[
-            pltpu.VMEM((n - 1, rows, width), jnp.bfloat16),
-            pltpu.VMEM((n - 1, rows, width), jnp.bfloat16),
-            pltpu.SemaphoreType.DMA((3, pieces, n - 1)),
-            pltpu.SemaphoreType.DMA((3, pieces, n - 1)),
-        ],
-        compiler_params=pltpu.CompilerParams(
-            collective_id=collective_id, has_side_effects=True, vmem_limit_bytes=VMEM_LIMIT
-        ),
-    )(gate.astype(jnp.bfloat16), up.astype(jnp.bfloat16), own_gate, own_up)
-    return out.reshape(tokens, width)
+    )(x, state, gate_weight, up_weight, down_weight)
 
 
 def local(
@@ -460,12 +663,7 @@
     state = residual + projected
     squares = lax.psum(jnp.sum(state * state, axis=1), "kvh")
     normed = (state * lax.rsqrt(squares / features + EPSILON)[:, None] * norm_gain).astype(jnp.bfloat16)
-    block_rows = gather_tokens(normed, 2)
-    gate_part = jnp.dot(block_rows, gate_weight, preferred_element_type=jnp.float32)
-    up_part = jnp.dot(block_rows, up_weight, preferred_element_type=jnp.float32)
-    activation = gated(gate_part, up_part, 3)
-    down_part = jnp.dot(activation, down_weight, preferred_element_type=jnp.float32)
-    return scatter_tokens(down_part, state, 4)
+    return feed_forward(normed, state, gate_weight, up_weight, down_weight, 2)
 
 
 def solution(mesh):

time: 318 us -> 233 us (0.73)
  matrix products: 46.3 us -> 5.79 us
  Pallas kernels: 196 us -> 166 us
  starting transfers between devices: 22.4 us -> 14.7 us
  waiting for transfers between devices: 7.69 us -> 0.01 us
  blocking collectives: 30.8 us -> 35.5 us
  local copies, waits for them, and re-layouts: 8.6 us -> 5.16 us
    dot_general x3 -> x0, matrix products: 40.5 us -> none  [the longest x1 14.5 us: local(): up_part = jnp.dot(block_rows, up_weight, preferred_element_type=jnp.float32)]
    pallas_call x2 -> x1, Pallas kernels: 81.5 us -> 52.1 us  [gather_tokens(): pl.pallas_call(functools.partial(gather_body, dims=dims, pieces=pieces),...]
    all_to_all x0 -> x1, blocking collectives: none -> 10.1 us  [local(): lax.all_to_all(regrouped, 'kvh', split_axis=1, concat_axis=0, tiled=True)]
    all_to_all x1 -> x0, waiting for transfers between devices: 7.68 us -> none  [local(): lax.all_to_all(regrouped, 'kvh', split_axis=1, concat_axis=0, tiled=True)]
    all_to_all x1, blocking collectives: 24.8 us -> 19.6 us  [local(): lax.all_to_all(partial_rows.astype(jnp.bfloat16), ('req', 'ffn'), split_a...]
    all_to_all x1, starting transfers between devices: 18.9 us -> 14.7 us  [local(): lax.all_to_all(own, 'ffn', split_axis=0, concat_axis=0, tiled=True)]
    all_to_all x1 -> x0, starting transfers between devices: 3.49 us -> none  [local(): lax.all_to_all(regrouped, 'kvh', split_axis=1, concat_axis=0, tiled=True)]
    pallas_call x2 -> x1, Pallas kernels: 109 us -> 108 us  [feed_forward(): pl.pallas_call(functools.partial(ffn_body, dims=(hn, ln, cn), kn=kn, rc=r...]
  transfers between devices with their start and end apart: 2 -> 1, of which waited for: 1 -> 0; matrix products, arithmetic and copies ran while one was open for 0% -> 1% of each run, Pallas kernels for 0% -> 0%
where the time goes in v1:
time: 233 us; the launch traced here: 231 us
  Pallas kernels  166 us (71%)
  blocking collectives  35.5 us (15%)
  starting transfers between devices  14.7 us (6%)
  matrix products  5.79 us (2%)
  local copies, waits for them, and re-layouts  5.16 us (2%)
  other arithmetic  2.73 us (1%)
    pallas_call x1, Pallas kernels, feed_forward(): pl.pallas_call(functools.partial(ffn_body, dims=(hn, ln, cn), kn=kn, rc=r...  108 us
    pallas_call x1, Pallas kernels, gather_tokens(): pl.pallas_call(functools.partial(gather_body, dims=dims, pieces=pieces),...  52.1 us
    all_to_all x1, blocking collectives, local(): lax.all_to_all(partial_rows.astype(jnp.bfloat16), ('req', 'ffn'), split_a...  19.6 us
    all_to_all x1, starting transfers between devices, local(): lax.all_to_all(own, 'ffn', split_axis=0, concat_axis=0, tiled=True)  14.7 us
    all_to_all x1, blocking collectives, local(): lax.all_to_all(regrouped, 'kvh', split_axis=1, concat_axis=0, tiled=True)  10.1 us
    pallas_call x1, Pallas kernels, attention_part(): pl.pallas_call(body, out_shape=(jax.ShapeDtypeStruct((nodes, width), jnp....  5.86 us
    dot_general x1, matrix products, local(): jnp.dot(gather_tokens(attention, 1), out_weight, preferred_element_type=j...  5.79 us
  transfers between devices with their start and end apart: 1, of which 0 were waited for; matrix products, arithmetic and copies ran while one was open for 1% of the time, Pallas kernels for 0%

profile of v1, /device:TPU:1, one launch (start us, length us, event | category | flops | bytes accessed | tf_op | source)
XLA Modules:
  0.0 231.0 jit_solution(5376576520048743780)
XLA Ops:
  0.0 1.3 dynamic_slice.7
  2.0 0.6 pad_add_fusion.len_ref
  2.6 5.9 %shard_map.127 = (bf16[64,4096]{1,0:T(8,128)(2,1)}, f32[4,2,512]{2,1,0:T(2,128)}) custom-call(s32[2]{0:T(128)} %pad_add_fusion.len_ref, bf16[64,4096]{1,0:T(8,128)(2,1)} %bitcast.35, bf16[64,512]{1,0:T(8,128)(2,1)} %bitcast.39, bf16[64,512]{1,0:T(8,128)(2,1)} %bitcast.40, bf16[4,4096,128]{2,1,0:T(8,128)(2,1)} %bitcast.31, bf16[4,4096,128]{2,1,0:T(8,128)(2,1)} %bitcast.32, ...), custom_call_target="tpu_custom_call" | custom-call | tf_op jit(solution)/shard_map/pallas_call | solution.py:89
  8.5 14.7 %all-to-all-start = ((bf16[2,32,4096]{2,1,0:T(8,128)(2,1)}), bf16[2,32,4096]{2,1,0:T(8,128)(2,1)S(1)}, u32[]{:S(2)}, u32[]{:S(2)}) async-start(bf16[2,32,4096]{2,1,0:T(8,128)(2,1)} %bitcast.36), calls=%async_computation | async-start | bytes 1048576 | tf_op jit(solution)/shard_map/all_to_all | solution.py:650
  23.1 2.0 all-gather
  25.2 0.1 slice_reduce_fusion
  25.3 0.1 sub.19
  25.4 0.1 div.17
  25.4 0.1 squeeze.36
  25.5 0.1 squeeze.37
  25.6 0.1 constant_dynamic-slice_fusion
  25.7 0.1 fusion.1
  25.8 0.1 copy.20
  25.9 0.3 mul.46
  26.2 0.2 mul.47
  26.4 0.0 all-to-all-done
  26.4 0.8 multiply_reduce_fusion.x_ref
  27.2 52.1 %shard_map.128 = bf16[4,2,2,32,4096]{4,3,2,1,0:T(8,128)(2,1)} custom-call(bf16[32,4096]{1,0:T(8,128)(2,1)} %multiply_reduce_fusion.x_ref), custom_call_target="tpu_custom_call" | custom-call | tf_op jit(solution)/shard_map/pallas_call | solution.py:215
  79.4 5.8 %convolution_convert_fusion = bf16[512,512]{1,0:T(8,128)(2,1)S(1)} fusion(bf16[512,4096]{1,0:T(8,128)(2,1)} %bitcast.33, bf16[4096,512]{1,0:T(8,128)(2,1)} %param.21), kind=kOutput, calls=%fused_computation | convolution fusion | flops 2147745792 | bytes 8912896 | tf_op jit(solution)/shard_map/dot_general | solution.py:657
  85.2 0.0 copy-start.1
  85.2 0.0 copy-start.2
  85.2 19.6 %all_to_all.38 = bf16[16,32,512]{2,1,0:T(8,128)(2,1)S(1)} all-to-all(bf16[16,32,512]{2,1,0:T(8,128)(2,1)S(1)} %bitcast.37), channel_id=1, replica_groups=mesh['req'=8,'kvh'=2,'ffn'=2] {'req','ffn'}, dimensions={0} | all-to-all | bytes 1048576 | tf_op jit(solution)/shard_map/all_to_all | solution.py:658
  104.8 0.3 copy.21
  105.1 0.4 all_to_all.33
  105.5 0.3 copy.22
  105.8 10.1 %all_to_all.39 = bf16[32,2,4096]{2,0,1:T(8,128)(2,1)S(1)} all-to-all(bf16[32,2,4096]{2,0,1:T(8,128)(2,1)S(1)} %copy.22), channel_id=1, replica_groups=mesh['req'=8,'kvh'=2,'ffn'=2] {'kvh'}, dimensions={1} | all-to-all | bytes 1048576 | tf_op jit(solution)/shard_map/all_to_all | solution.py:661
  115.9 0.1 convert_reduce_fusion
  116.0 0.2 multiply_reduce_fusion.1
  116.2 3.8 %psum.7 = f32[32]{0:T(128)S(1)} all-reduce(f32[32]{0:T(128)S(1)} %get-tuple-element.11), channel_id=1, replica_groups=mesh['req'=8,'kvh'=2,'ffn'=2] {'kvh'}, use_global_device_ids=true, to_apply=%region_5.6 | all-reduce | flops 32 | bytes 256 | tf_op jit(solution)/shard_map/psum | solution.py:664
  120.0 0.8 multiply_convert_fusion.x_ref
  120.8 108.3 %shard_map.129 = f32[32,4096]{1,0:T(8,128)} custom-call(bf16[32,4096]{1,0:T(8,128)(2,1)} %multiply_convert_fusion.x_ref, f32[32,4096]{1,0:T(8,128)} %copy-done, bf16[4096,1792]{1,0:T(8,128)(2,1)} %gate_hbm.1, bf16[4096,1792]{1,0:T(8,128)(2,1)} %up_hbm.1, bf16[1792,4096]{1,0:T(8,128)(2,1)} %down_hbm.1), custom_call_target="tpu_custom_call" | custom-call | tf_op jit(solution)/shard_map/pallas_call | solution.py:578
  229.1 1.9 copy.28
  (7 shorter events, 0.0 us)
Async XLA Ops:
  8.5 17.9 %all-to-all-start = ((bf16[2,32,4096]{2,1,0:T(8,128)(2,1)}), bf16[2,32,4096]{2,1,0:T(8,128)(2,1)S(1)}, u32[]{:S(2)}, u32[]{:S(2)}) async-start(bf16[2,32,4096]{2,1,0:T(8,128)(2,1)} %bitcast.36), calls=%async_computation | async-start | bytes 1048576 | tf_op jit(solution)/shard_map/all_to_all | solution.py:650
  85.2 30.8 %copy-start.1 = (f32[32,4096]{1,0:T(8,128)S(1)}, f32[32,4096]{1,0:T(8,128)}, u32[]{:S(2)}) copy-start(f32[32,4096]{1,0:T(8,128)} %param.20) | copy-start | bytes 1572868
  85.2 34.8 %copy-start.2 = (f32[4096]{0:T(1024)S(1)}, f32[4096]{0:T(1024)}, u32[]{:S(2)}) copy-start(f32[4096]{0:T(1024)} %param.22) | copy-start | bytes 49156
  116.2 4.6 %copy-start = (f32[32,4096]{1,0:T(8,128)}, f32[32,4096]{1,0:T(8,128)S(1)}, u32[]{:S(2)}) copy-start(f32[32,4096]{1,0:T(8,128)S(1)} %get-tuple-element.12.state_ref) | copy-start | bytes 1572868

commit v2 on v1

--- a/solution.py
+++ b/solution.py
@@ -10,110 +10,6 @@
 
 MASKED = -1e30
 EPSILON = 1e-05
-
-
-def attend(len_ref, q_ref, tk_ref, tv_ref, k_ref, v_ref, par_ref, o_ref, ml_ref, acc, stat, *, chunk, factor):
-    live = len_ref[0]
-    tree_live = len_ref[1]
-    nodes = q_ref.shape[0]
-    size = k_ref.shape[-1]
-    group = q_ref.shape[1] // size
-    rows = nodes * group
-    q = jnp.concatenate([q_ref[:, g * size : (g + 1) * size] for g in range(group)], axis=0)
-    acc[...] = jnp.zeros_like(acc)
-    stat[0:1, :] = jnp.full((1, rows), MASKED, jnp.float32)
-    stat[1:2, :] = jnp.zeros((1, rows), jnp.float32)
-
-    def scores_of(keys):
-        return lax.dot_general(keys, q, (((1,), (1,)), ((), ())), preferred_element_type=jnp.float32)
-
-    def absorb(scores, usable, values):
-        if usable is not None:
-            scores = jnp.where(usable, scores, MASKED)
-        old = stat[0:1, :]
-        top = jnp.maximum(old, jnp.max(scores, axis=0, keepdims=True))
-        weights = jnp.exp2(scores * factor - top * factor)
-        if usable is not None:
-            weights = jnp.where(usable, weights, 0.0)
-        shrink = jnp.exp2((old - top) * factor)
-        stat[0:1, :] = top
-        stat[1:2, :] = stat[1:2, :] * shrink + jnp.sum(weights, axis=0, keepdims=True)
-        acc[...] = acc[...] * shrink + lax.dot_general(
-            values, weights.astype(jnp.bfloat16), (((0,), (0,)), ((), ())), preferred_element_type=jnp.float32
-        )
-
-    full = live // chunk
-
-    def visit(c, carry):
-        at = pl.ds(pl.multiple_of(c * chunk, chunk), chunk)
-        absorb(scores_of(k_ref[0, at, :]), None, v_ref[0, at, :])
-        return carry
-
-    lax.fori_loop(0, full, visit, 0)
-
-    @pl.when(live > full * chunk)
-    def _():
-        at = pl.ds(pl.multiple_of(full * chunk, chunk), chunk)
-        spot = full * chunk + lax.broadcasted_iota(jnp.int32, (chunk, rows), 0)
-        absorb(scores_of(k_ref[0, at, :]), spot < live, v_ref[0, at, :])
-
-    @pl.when(tree_live > 0)
-    def _():
-        up = lax.broadcasted_iota(jnp.int32, (nodes, nodes), 0)
-        across = lax.broadcasted_iota(jnp.int32, (nodes, nodes), 1)
-        link = jnp.where(up == par_ref[...], 1.0, 0.0) + jnp.where(up == across, 1.0, 0.0)
-        reach = jnp.minimum(link, 1.0)
-        for _ in range((nodes - 1).bit_length()):
-            half = reach.astype(jnp.bfloat16)
-            reach = jnp.minimum(jnp.dot(half, half, preferred_element_type=jnp.float32), 1.0)
-        row = lax.broadcasted_iota(jnp.int32, (nodes, rows), 0)
-        col = lax.broadcasted_iota(jnp.int32, (nodes, rows), 1)
-        spread = jnp.where(lax.rem(col, nodes) == row, 1.0, 0.0).astype(jnp.bfloat16)
-        mask = jnp.dot(reach.astype(jnp.bfloat16), spread, preferred_element_type=jnp.float32)
-        absorb(scores_of(tk_ref[...]), mask > 0.5, tv_ref[...])
-
-    total = stat[1:2, :]
-    out = (acc[...] / jnp.where(total > 0.0, total, 1.0)).T.astype(jnp.bfloat16)
-    for g in range(group):
-        o_ref[:, g * size : (g + 1) * size] = out[g * nodes : (g + 1) * nodes, :]
-    ml_ref[0] = jnp.concatenate([stat[0:1, :] * (size**-0.5), total], axis=0)
-
-
-def attention_part(queries, tree_keys, tree_values, keys, values, lengths2, parents):
-    heads, span, size = keys.shape
-    nodes, width = queries.shape
-    wide = width // heads
-    rows = wide // size * nodes
-    chunk = math.gcd(span, 1024)
-    body = functools.partial(attend, chunk=chunk, factor=size**-0.5 * math.log2(math.e))
-    return pl.pallas_call(
-        body,
-        out_shape=(
-            jax.ShapeDtypeStruct((nodes, width), jnp.bfloat16),
-            jax.ShapeDtypeStruct((heads, 2, rows), jnp.float32),
-        ),
-        grid_spec=pltpu.PrefetchScalarGridSpec(
-            num_scalar_prefetch=1,
-            grid=(heads,),
-            in_specs=[
-                pl.BlockSpec((nodes, wide), lambda h, n: (0, h)),
-                pl.BlockSpec((nodes, size), lambda h, n: (0, h)),
-                pl.BlockSpec((nodes, size), lambda h, n: (0, h)),
-                pl.BlockSpec((1, span, size), lambda h, n: (h, 0, 0)),
-                pl.BlockSpec((1, span, size), lambda h, n: (h, 0, 0)),
-                pl.BlockSpec((1, nodes), lambda h, n: (0, 0)),
-            ],
-            out_specs=(
-                pl.BlockSpec((nodes, wide), lambda h, n: (0, h)),
-                pl.BlockSpec((1, 2, rows), lambda h, n: (h, 0, 0)),
-            ),
-            scratch_shapes=[
-                pltpu.VMEM((size, rows), jnp.float32),
-                pltpu.VMEM((8, rows), jnp.float32),
-            ],
-        ),
-        compiler_params=pltpu.CompilerParams(dimension_semantics=("arbitrary",)),
-    )(lengths2, queries, tree_keys, tree_values, keys, values, parents)
 
 
 MESH = pl.DeviceIdType.MESH
@@ -153,80 +49,402 @@
     )
 
 
-def gather_body(x_ref, out_ref, send, recv, own_sem, *, dims, pieces):
-    hi_n, lo_n, core_n = dims
-    hi, lo, core, hi_peers, lo_peers, core_peers = staged_places(*dims)
-    wide = x_ref.shape[1] // pieces
-    meet(hi_peers + lo_peers + core_peers)
-    own = pltpu.make_async_copy(x_ref, out_ref.at[hi, lo, core], own_sem)
-    own.start()
-    first, second, third = [], [], []
-    for p in range(pieces):
-        cols = pl.ds(p * wide, wide)
-        group = []
-        for d, (_, where) in enumerate(hi_peers):
-            copy = remote(
-                x_ref.at[:, cols], out_ref.at[hi, lo, core, :, cols], send.at[p, d], recv.at[p, d], where
+def token_gather(dims, rc, source, target, send, recv, own_sem):
+    hn, ln, cn = dims
+    req = lax.axis_index("req")
+    hi, lo, core = req // ln, lax.rem(req, ln), lax.axis_index("ffn")
+    to_hi = lambda d: {"req": lax.rem(hi + d, hn) * ln + lo}
+    to_lo = lambda d: {"req": hi * ln + lax.rem(lo + d, ln)}
+    to_core = lambda d: {"ffn": lax.rem(core + d, cn)}
+    hi_order = sorted(range(1, hn), key=lambda d: min(d, hn - d))
+    base_lo = hn - 1
+    base_core = base_lo + hn * (ln - 1)
+
+    def place(c, e, g):
+        b = (core * ln + lax.rem(lo + ln - g, ln)) * hn + lax.rem(hi + hn - e, hn)
+        return target(c, pl.ds(pl.multiple_of(b * rc, rc), rc))
+
+    def hi_copy(c, d):
+        at = d - 1
+        return remote(source(c), place(c, 0, 0), send.at[c, at], recv.at[c, at], to_hi(d))
+
+    def lo_copy(c, e, d):
+        at = base_lo + e * (ln - 1) + d - 1
+        src = source(c) if e == 0 else place(c, e, 0)
+        return remote(src, place(c, e, 0), send.at[c, at], recv.at[c, at], to_lo(d))
+
+    def core_copy(c, e, g, d):
+        at = base_core + (e * ln + g) * (cn - 1) + d - 1
+        src = source(c) if e == 0 and g == 0 else place(c, e, g)
+        return remote(src, place(c, e, g), send.at[c, at], recv.at[c, at], to_core(d))
+
+    def own_copy(c):
+        return pltpu.make_async_copy(source(c), place(c, 0, 0), own_sem.at[c])
+
+    def start(c):
+        for d in hi_order:
+            hi_copy(c, d).start()
+        for d in range(1, ln):
+            lo_copy(c, 0, d).start()
+        for d in range(1, cn):
+            core_copy(c, 0, 0, d).start()
+        own_copy(c).start()
+
+    def pass_hi(c):
+        for e in hi_order:
+            hi_copy(c, e).wait_recv()
+            for d in range(1, ln):
+                lo_copy(c, e, d).start()
+            for d in range(1, cn):
+                core_copy(c, e, 0, d).start()
+
+    def pass_lo(c):
+        for e in [0] + hi_order:
+            for g in range(1, ln):
+                lo_copy(c, e, g).wait_recv()
+                for d in range(1, cn):
+                    core_copy(c, e, g, d).start()
+
+    def finish(c):
+        for e in [0] + hi_order:
+            for g in range(ln):
+                for d in range(1, cn):
+                    core_copy(c, e, g, d).wait_recv()
+        own_copy(c).wait()
+
+    def sent(c):
+        for d in range(1, hn):
+            hi_copy(c, d).wait_send()
+        for e in range(hn):
+            for d in range(1, ln):
+                lo_copy(c, e, d).wait_send()
+            for g in range(ln):
+                for d in range(1, cn):
+                    core_copy(c, e, g, d).wait_send()
+
+    return start, pass_hi, pass_lo, finish, sent
+
+
+def gather_links(dims):
+    hn, ln, cn = dims
+    return (hn - 1) + hn * (ln - 1) + hn * ln * (cn - 1)
+
+
+def front_body(
+    len_ref, q_ref, tk_ref, tv_ref, k_hbm, v_hbm, par_ref, res_ref, gain_ref, wo_hbm, state_ref, normed_ref,
+    kbuf, vbuf, wo, tree_mask, sbuf, half_own, half_got, attn, gath, proj, pack, blocks_got, cross_got, squares, squares_got,
+    k_sem, v_sem, wo_sem, own_sem, x_send, x_recv, g_send, g_recv, b_send, b_recv, c_send, c_recv, s_send, s_recv,
+    *, dims, kn, features,
+):
+    hn, ln, cn = dims
+    n = hn * ln * cn
+    hi, lo, core, _, _, _ = staged_places(*dims)
+    k = lax.axis_index("kvh")
+    heads, span, size = kbuf.shape
+    nodes = q_ref.shape[0]
+    group = q_ref.shape[1] // (heads * size)
+    rows = group * nodes
+    mine = nodes // cn
+    part_rows = group * mine
+    fb = pack.shape[1]
+    per = n // kn
+    factor = size**-0.5 * math.log2(math.e)
+    chunk = math.gcd(span, 1024)
+    to_core = lambda d: {"ffn": lax.rem(core + d, cn)}
+    to_kvh = lambda d: {"kvh": lax.rem(k + d, kn)}
+    flat = [(e, g, d) for e in range(hn) for g in range(ln) for d in range(cn)]
+
+    def plane(e, g, d):
+        return {"req": lax.rem(hi + e, hn) * ln + lax.rem(lo + g, ln), "ffn": lax.rem(core + d, cn)}
+
+    meet(
+        [(0, plane(*t)) for t in flat[1:]] + [(0, to_kvh(d)) for d in range(1, kn)]
+    )
+    k_copy = lambda h: pltpu.make_async_copy(k_hbm.at[h], kbuf.at[h], k_sem.at[h])
+    v_copy = lambda h: pltpu.make_async_copy(v_hbm.at[h], vbuf.at[h], v_sem.at[h])
+    wo_copy = pltpu.make_async_copy(wo_hbm, wo, wo_sem)
+    for h in range(heads):
+        k_copy(h).start()
+        v_copy(h).start()
+    wo_copy.start()
+    live = jnp.clip(len_ref[lax.axis_index("req")] - core * span, 0, span)
+
+    up = lax.broadcasted_iota(jnp.int32, (nodes, nodes), 0)
+    across = lax.broadcasted_iota(jnp.int32, (nodes, nodes), 1)
+    eye = jnp.where(up == across, 1.0, 0.0).astype(jnp.bfloat16)
+    link = jnp.where(up == par_ref[...], 1.0, 0.0).astype(jnp.bfloat16)
+    over = lax.dot_general(link, eye, (((0,), (0,)), ((), ())), preferred_element_type=jnp.float32)
+    reach = jnp.minimum(over + jnp.where(up == across, 1.0, 0.0), 1.0)
+    for _ in range((nodes - 1).bit_length()):
+        half = reach.astype(jnp.bfloat16)
+        reach = jnp.minimum(jnp.dot(half, half, preferred_element_type=jnp.float32), 1.0)
+    reach = reach * jnp.where(core == 0, 1.0, 0.0)
+    tree_mask[...] = jnp.concatenate(
+        [reach[f * mine : (f + 1) * mine] for f in range(cn) for _ in range(group)], axis=0
+    )
+
+    def head_cols(h):
+        return pl.ds(pl.multiple_of(h * size, size), size)
+
+    def queries_of(h):
+        return jnp.concatenate(
+            [
+                q_ref[f * mine : (f + 1) * mine, pl.ds(pl.multiple_of((h * group + g) * size, size), size)]
+                for f in range(cn)
+                for g in range(group)
+            ],
+            axis=0,
+        )
+
+    def tree_scores(h):
+        s = lax.dot_general(
+            queries_of(h), tk_ref[:, head_cols(h)], (((1,), (1,)), ((), ())), preferred_element_type=jnp.float32
+        )
+        return jnp.where(tree_mask[...] > 0.5, s, MASKED)
+
+    def score(h):
+        k_copy(h).wait()
+        q = queries_of(h)
+        first = kbuf[h, pl.ds(0, 16), :].astype(jnp.float32)[0:1]
+        top = jnp.max(tree_scores(h), axis=1, keepdims=True)
+        for c in range(span // chunk):
+            spot = c * chunk + lax.broadcasted_iota(jnp.int32, (chunk, size), 0)
+            keys = jnp.where(spot < live, kbuf[h, pl.ds(c * chunk, chunk), :].astype(jnp.float32), first)
+            s = lax.dot_general(
+                q, keys.astype(jnp.bfloat16), (((1,), (1,)), ((), ())), preferred_element_type=jnp.float32
             )
-            copy.start()
-            group.append(copy)
-        first.append(group)
-    own.wait()
-    base = len(hi_peers)
-    for step in range(pieces + 1):
-        if step < pieces:
-            cols = pl.ds(step * wide, wide)
-            for copy in first[step]:
-                copy.wait_recv()
-            group = []
-            for d, (_, where) in enumerate(lo_peers):
-                part = out_ref.at[:, lo, core, :, cols]
-                copy = remote(part, part, send.at[step, base + d], recv.at[step, base + d], where)
-                copy.start()
-                group.append(copy)
-            second.append(group)
-        if step > 0:
-            p = step - 1
-            cols = pl.ds(p * wide, wide)
-            for copy in second[p]:
-                copy.wait_recv()
-            group = []
-            for d, (_, where) in enumerate(core_peers):
-                at = base + len(lo_peers) + d
-                part = out_ref.at[:, :, core, :, cols]
-                copy = remote(part, part, send.at[p, at], recv.at[p, at], where)
-                copy.start()
-                group.append(copy)
-            third.append(group)
-    for group in third:
-        for copy in group:
-            copy.wait_recv()
-    for group in first + second + third:
-        for copy in group:
-            copy.wait_send()
-
-
-def gather_tokens(x, collective_id):
+            sbuf[:, pl.ds(c * chunk, chunk)] = s
+            top = jnp.maximum(top, jnp.max(s, axis=1, keepdims=True))
+        half_own[h, :, pl.ds(size, size)] = jnp.broadcast_to(top, (rows, size))
+
+    def weigh(h):
+        v_copy(h).wait()
+        top = half_own[h, :, pl.ds(size, 1)]
+        usable = tree_mask[...] > 0.5
+        w = jnp.where(usable, jnp.exp2((tree_scores(h) - top) * factor), 0.0).astype(jnp.bfloat16)
+        ones = jnp.ones((nodes, size), jnp.bfloat16)
+        total = jnp.dot(
+            w, jnp.concatenate([tv_ref[:, head_cols(h)], ones], axis=1), preferred_element_type=jnp.float32
+        )
+        for c in range(span // chunk):
+            spot = c * chunk + lax.broadcasted_iota(jnp.int32, (chunk, size), 0)
+            usable = spot < live
+            values = jnp.where(usable, vbuf[h, pl.ds(c * chunk, chunk), :].astype(jnp.float32), 0.0)
+            count = jnp.where(usable, 1.0, 0.0)
+            both = jnp.concatenate([values.astype(jnp.bfloat16), count.astype(jnp.bfloat16)], axis=1)
+            w = jnp.exp2((sbuf[:, pl.ds(c * chunk, chunk)] - top) * factor).astype(jnp.bfloat16)
+            total = total + jnp.dot(w, both, preferred_element_type=jnp.float32)
+        seen = jnp.where((live > 0) | (core == 0), 1.0, 0.0)
+        top = jnp.where(seen > 0.5, top * factor, MASKED)
+        lane = lax.broadcasted_iota(jnp.int32, (rows, size), 1)
+        half_own[h, :, pl.ds(0, size)] = total[:, :size]
+        half_own[h, :, pl.ds(size, size)] = jnp.where(lane < size // 2, total[:, size:], top)
+        for d in range(1, cn):
+            half_copy(h, d).start()
+
+    def part_of(f):
+        return pl.ds(pl.multiple_of(f * part_rows, part_rows), part_rows)
+
+    def half_copy(h, d):
+        src = half_own.at[h, part_of(lax.rem(core + d, cn)), :]
+        return remote(src, half_got.at[h, d - 1], x_send.at[h, d - 1], x_recv.at[h, d - 1], to_core(d))
+
+    def merge(h):
+        for d in range(1, cn):
+            half_copy(h, d).wait_recv()
+        pieces = [half_own[h, part_of(core), :]] + [half_got[h, d] for d in range(cn - 1)]
+        tops = [p[:, size + size // 2 : size + size // 2 + 1] for p in pieces]
+        best = functools.reduce(jnp.maximum, tops)
+        above, below = 0.0, 0.0
+        for p, t in zip(pieces, tops):
+            scale = jnp.exp2(t - best)
+            above = above + p[:, :size] * scale
+            below = below + p[:, size : size + 1] * scale
+        result = (above / below).astype(jnp.bfloat16)
+        for g in range(group):
+            attn[h, :, pl.ds(g * size, size)] = result[g * mine : (g + 1) * mine]
+
+    start, pass_hi, pass_lo, finish, sent = token_gather(
+        dims, mine, lambda h: attn.at[h], lambda h, r: gath.at[h, r, :], g_send, g_recv, own_sem
+    )
+
+    def project(h):
+        wide = group * size
+        piece = jnp.dot(
+            gath[h], wo[pl.ds(pl.multiple_of(h * wide, wide), wide), :], preferred_element_type=jnp.float32
+        )
+
+        @pl.when(h == 0)
+        def _():
+            proj[...] = piece
+
+        @pl.when(h > 0)
+        def _():
+            proj[...] = proj[...] + piece
+
+    def guarded(h, *stages):
+        @pl.when((h >= 0) & (h < heads))
+        def _():
+            for stage in stages:
+                stage(h)
+
+    def step(i, carry):
+        guarded(i, score)
+        guarded(i - 1, merge, start)
+        guarded(i - 2, pass_hi)
+        guarded(i, weigh)
+        guarded(i - 2, pass_lo)
+
+        @pl.when(i == 2)
+        def _():
+            wo_copy.wait()
+
+        guarded(i - 3, finish, project)
+        return carry
+
+    lax.fori_loop(0, heads + 3, step, 0)
+    pack[...] = proj[...].astype(jnp.bfloat16)
+
+    def rows_at(e, g, d):
+        b = (lax.rem(core + d, cn) * ln + lax.rem(lo + g, ln)) * hn + lax.rem(hi + e, hn)
+        return pl.ds(pl.multiple_of(b * mine, mine), mine)
+
+    def block_copy(t):
+        e, g, d = flat[t]
+        return remote(pack.at[rows_at(e, g, d), :], blocks_got.at[t], b_send.at[t], b_recv.at[t], plane(e, g, d))
+
+    far_first = sorted(range(1, n), key=lambda t: -min(flat[t][0], hn - flat[t][0]))
+    for t in far_first:
+        block_copy(t).start()
+    blocks_got[0] = pack[rows_at(0, 0, 0), :]
+
+    def origin(b):
+        f, r = lax.rem(b, cn), lax.div(b, cn)
+        h, l = lax.div(r, ln), lax.rem(r, ln)
+        return (lax.rem(hi + hn - h, hn) * ln + lax.rem(lo + ln - l, ln)) * cn + lax.rem(core + cn - f, cn)
+
+    def arrived(t):
+        @pl.when(t > 0)
+        def _():
+            remote(
+                pack.at[pl.ds(0, mine), :], blocks_got.at[t], b_send.at[t], b_recv.at[t], to_core(1)
+            ).wait_recv()
+
+    def cross_copy(d, t):
+        return remote(blocks_got.at[t], cross_got.at[d - 1, t], c_send.at[d - 1, t], c_recv.at[d - 1, t], to_kvh(d))
+
+    for d in range(1, kn):
+
+        def forward(j, carry, d=d):
+            t = origin(lax.rem(k + d, kn) * per + j)
+            arrived(t)
+            cross_copy(d, t).start()
+            return carry
+
+        lax.fori_loop(0, per, forward, 0)
+
+    def collect(j, square):
+        t = origin(k * per + j)
+        arrived(t)
+        total = blocks_got[t].astype(jnp.float32)
+        for d in range(1, kn):
+            cross_copy(d, t).wait_recv()
+            total = total + cross_got[d - 1, t].astype(jnp.float32)
+        cols = pl.ds(pl.multiple_of(j * fb, fb), fb)
+        total = total + res_ref[:, cols]
+        state_ref[:, cols] = total
+        return square + jnp.sum(total * total, axis=1, keepdims=True)
+
+    square = lax.fori_loop(0, per, collect, jnp.zeros((mine, 1), jnp.float32))
+    squares[...] = jnp.broadcast_to(square, squares.shape)
+
+    def square_copy(d):
+        return remote(squares, squares_got.at[d - 1], s_send.at[d - 1], s_recv.at[d - 1], to_kvh(d))
+
+    for d in range(1, kn):
+        square_copy(d).start()
+    for d in range(1, kn):
+        square_copy(d).wait_recv()
+        square = square + squares_got[d - 1, :, pl.ds(0, 1)]
+    scale = lax.rsqrt(square / features + EPSILON)
+
+    def norm(j, carry):
+        cols = pl.ds(pl.multiple_of(j * fb, fb), fb)
+        normed_ref[:, cols] = (state_ref[:, cols] * scale * gain_ref[:, cols]).astype(jnp.bfloat16)
+        return carry
+
+    lax.fori_loop(0, per, norm, 0)
+    for h in range(heads):
+        sent(h)
+        for d in range(1, cn):
+            half_copy(h, d).wait_send()
+    for t in range(1, n):
+        block_copy(t).wait_send()
+    for d in range(1, kn):
+
+        def cross_sent(j, carry, d=d):
+            cross_copy(d, origin(lax.rem(k + d, kn) * per + j)).wait_send()
+            return carry
+
+        lax.fori_loop(0, per, cross_sent, 0)
+        square_copy(d).wait_send()
+
+
+def front(queries, tree_keys, tree_values, keys, values, lengths, parents, residual, out_weight, norm_gain, collective_id):
     dims = (*split_count(lax.axis_size("req")), lax.axis_size("ffn"))
-    rows, width = x.shape
-    pieces = math.gcd(width // 128, 4)
-    links = sum(dims) - 3
+    cn, kn = dims[2], lax.axis_size("kvh")
+    n = math.prod(dims)
+    heads, span, size = keys.shape
+    nodes, width = queries.shape
+    wide = width // heads
+    rows = wide // size * nodes
+    mine = residual.shape[0]
+    fb = out_weight.shape[1]
+    links = gather_links(dims)
     vmem = pl.BlockSpec(memory_space=pltpu.VMEM)
-    out = pl.pallas_call(
-        functools.partial(gather_body, dims=dims, pieces=pieces),
-        out_shape=jax.ShapeDtypeStruct((*dims, rows, width), x.dtype),
-        in_specs=[vmem],
-        out_specs=vmem,
+    hbm = pl.BlockSpec(memory_space=pl.ANY)
+    f32, b16 = jnp.float32, jnp.bfloat16
+    dma = pltpu.SemaphoreType.DMA
+    return pl.pallas_call(
+        functools.partial(front_body, dims=dims, kn=kn, features=norm_gain.shape[0] * kn),
+        out_shape=(jax.ShapeDtypeStruct(residual.shape, f32), jax.ShapeDtypeStruct(residual.shape, b16)),
+        in_specs=[pl.BlockSpec(memory_space=pltpu.SMEM), vmem, vmem, vmem, hbm, hbm, vmem, vmem, vmem, hbm],
+        out_specs=(vmem, vmem),
         scratch_shapes=[
-            pltpu.SemaphoreType.DMA((pieces, links)),
-            pltpu.SemaphoreType.DMA((pieces, links)),
-            pltpu.SemaphoreType.DMA,
+            pltpu.VMEM((heads, span, size), b16),
+            pltpu.VMEM((heads, span, size), b16),
+            pltpu.VMEM(out_weight.shape, b16),
+            pltpu.VMEM((rows, nodes), f32),
+            pltpu.VMEM((rows, span), f32),
+            pltpu.VMEM((heads, rows, 2 * size), f32),
+            pltpu.VMEM((heads, cn - 1, rows // cn, 2 * size), f32),
+            pltpu.VMEM((heads, mine, wide), b16),
+            pltpu.VMEM((heads, n * mine, wide), b16),
+            pltpu.VMEM((n * mine, fb), f32),
+            pltpu.VMEM((n * mine, fb), b16),
+            pltpu.VMEM((n, mine, fb), b16),
+            pltpu.VMEM((kn - 1, n, mine, fb), b16),
+            pltpu.VMEM((mine, 128), f32),
+            pltpu.VMEM((kn - 1, mine, 128), f32),
+            dma((heads,)),
+            dma((heads,)),
+            dma,
+            dma((heads,)),
+            dma((heads, cn - 1)),
+            dma((heads, cn - 1)),
+            dma((heads, links)),
+            dma((heads, links)),
+            dma((n,)),
+            dma((n,)),
+            dma((kn - 1, n)),
+            dma((kn - 1, n)),
+            dma((kn - 1,)),
+            dma((kn - 1,)),
         ],
         compiler_params=pltpu.CompilerParams(
-            collective_id=collective_id, has_side_effects=True, vmem_limit_bytes=VMEM_LIMIT
+            collective_id=collective_id, has_side_effects=True, vmem_limit_bytes=63 * 1024 * 1024
         ),
-    )(x)
-    return out.reshape(math.prod(dims) * rows, width)
+    )(lengths, queries, tree_keys, tree_values, keys, values, parents, residual, norm_gain[None, :], out_weight)
 
 
 def lane_block(width, most):
@@ -274,75 +492,9 @@
         cols = pl.ds(pl.multiple_of(lax.rem(j, fs) * fw, fw), fw)
         return pltpu.make_async_copy(down_hbm.at[:, cols], wd.at[slot], wd_sem.at[slot])
 
-    def rows_of(h, b, c):
-        return pl.ds(pl.multiple_of(((c * ln + b) * hn + h) * rc, rc), rc)
-
-    def place(c, e, g, f):
-        return gath.at[c, rows_of(lax.rem(hi + hn - e, hn), lax.rem(lo + ln - g, ln), f), :]
-
-    base_lo = hn - 1
-    base_core = base_lo + hn * (ln - 1)
-
-    def hi_copy(c, d):
-        at = d - 1
-        src = x_ref.at[pl.ds(c * rc, rc), :]
-        return remote(src, place(c, 0, 0, core), g_send.at[c, at], g_recv.at[c, at], to_hi(d)[1])
-
-    def lo_copy(c, e, d):
-        at = base_lo + e * (ln - 1) + d - 1
-        src = x_ref.at[pl.ds(c * rc, rc), :] if e == 0 else place(c, e, 0, core)
-        return remote(src, place(c, e, 0, core), g_send.at[c, at], g_recv.at[c, at], to_lo(d)[1])
-
-    def core_copy(c, e, g, d):
-        at = base_core + (e * ln + g) * (cn - 1) + d - 1
-        src = x_ref.at[pl.ds(c * rc, rc), :] if e == 0 and g == 0 else place(c, e, g, core)
-        return remote(src, place(c, e, g, core), g_send.at[c, at], g_recv.at[c, at], to_core(d)[1])
-
-    hi_order = sorted(range(1, hn), key=lambda d: min(d, hn - d))
-
-    def own_copy(c):
-        return pltpu.make_async_copy(x_ref.at[pl.ds(c * rc, rc), :], place(c, 0, 0, core), own_sem.at[c])
-
-    def gather_start(c):
-        for d in hi_order:
-            hi_copy(c, d).start()
-        for d in range(1, ln):
-            lo_copy(c, 0, d).start()
-        for d in range(1, cn):
-            core_copy(c, 0, 0, d).start()
-        own_copy(c).start()
-
-    def gather_hi(c):
-        for e in hi_order:
-            hi_copy(c, e).wait_recv()
-            for d in range(1, ln):
-                lo_copy(c, e, d).start()
-            for d in range(1, cn):
-                core_copy(c, e, 0, d).start()
-
-    def gather_lo(c):
-        for e in [0] + hi_order:
-            for g in range(1, ln):
-                lo_copy(c, e, g).wait_recv()
-                for d in range(1, cn):
-                    core_copy(c, e, g, d).start()
-
-    def gather_end(c):
-        for e in [0] + hi_order:
-            for g in range(ln):
-                for d in range(1, cn):
-                    core_copy(c, e, g, d).wait_recv()
-        own_copy(c).wait()
-
-    def gather_sent(c):
-        for d in range(1, hn):
-            hi_copy(c, d).wait_send()
-        for e in range(hn):
-            for d in range(1, ln):
-                lo_copy(c, e, d).wait_send()
-            for g in range(ln):
-                for d in range(1, cn):
-                    core_copy(c, e, g, d).wait_send()
+    gather_start, gather_hi, gather_lo, gather_end, gather_sent = token_gather(
+        dims, rc, lambda c: x_ref.at[pl.ds(c * rc, rc), :], lambda c, r: gath.at[c, r, :], g_send, g_recv, own_sem
+    )
 
     def part_copy(s, d):
         return remote(part.at[s, d - 1], got.at[s, d - 1], p_send.at[s, d - 1], p_recv.at[s, d - 1], to_kvh(d)[1])
@@ -569,7 +721,7 @@
     pieces = chunks * (width // fw)
     tokens = hn * ln * cn * rc
     keep = tokens // kn
-    links = (hn - 1) + hn * (ln - 1) + hn * ln * (cn - 1)
+    links = gather_links((hn, ln, cn))
     vmem = pl.BlockSpec(memory_space=pltpu.VMEM)
     hbm = pl.BlockSpec(memory_space=pl.ANY)
     f32, b16 = jnp.float32, jnp.bfloat16
@@ -633,36 +785,19 @@
     up_weight,
     down_weight,
 ):
-    heads, half_len, size = cache_keys.shape[1:]
-    nodes = queries.shape[1]
-    group = queries.shape[2] // (heads * size)
-    request_index = lax.axis_index("req")
-    half_index = lax.axis_index("ffn")
-    halves = lax.axis_size("ffn")
-    features = norm_gain.shape[0] * lax.axis_size("kvh")
-    length = lax.dynamic_index_in_dim(lengths, request_index, keepdims=False)
-    live_len = jnp.clip(length - half_index * half_len, 0, half_len)
-    lengths2 = jnp.stack([live_len, (half_index == 0).astype(jnp.int32)])
-    own, ml = attention_part(
-        queries[0], tree_keys[0], tree_token_values[0], cache_keys[0], cached_value_rows[0], lengths2, parents
+    state, normed = front(
+        queries[0],
+        tree_keys[0],
+        tree_token_values[0],
+        cache_keys[0],
+        cached_value_rows[0],
+        lengths,
+        parents,
+        residual,
+        out_weight,
+        norm_gain,
+        1,
     )
-    mine_rows = nodes // halves
-    pair = lax.all_to_all(own, "ffn", split_axis=0, concat_axis=0, tiled=True).reshape(halves, mine_rows, -1)
-    ml_pair = lax.all_gather(ml, "ffn")
-    weights = ml_pair[:, :, 1] * jnp.exp(ml_pair[:, :, 0] - jnp.max(ml_pair[:, :, 0], axis=0))
-    share = (weights / jnp.sum(weights, axis=0)).reshape(halves, heads * group, nodes)
-    share = lax.dynamic_slice_in_dim(share, half_index * mine_rows, mine_rows, 2).transpose(0, 2, 1)[..., None]
-    mixed = jnp.sum(pair.astype(jnp.float32).reshape(halves, mine_rows, heads * group, size) * share, axis=0)
-    attention = mixed.astype(jnp.bfloat16).reshape(mine_rows, heads * group * size)
-    partial_rows = jnp.dot(gather_tokens(attention, 1), out_weight, preferred_element_type=jnp.float32)
-    regrouped = lax.all_to_all(
-        partial_rows.astype(jnp.bfloat16), ("req", "ffn"), split_axis=0, concat_axis=1, tiled=True
-    )
-    shares = lax.all_to_all(regrouped, "kvh", split_axis=1, concat_axis=0, tiled=True)
-    projected = jnp.sum(shares.astype(jnp.float32).reshape(-1, *residual.shape), axis=0)
-    state = residual + projected
-    squares = lax.psum(jnp.sum(state * state, axis=1), "kvh")
-    normed = (state * lax.rsqrt(squares / features + EPSILON)[:, None] * norm_gain).astype(jnp.bfloat16)
     return feed_forward(normed, state, gate_weight, up_weight, down_weight, 2)
 
 

time: 233 us -> 187 us (0.80)
  blocking collectives: 35.5 us -> 0 us
  Pallas kernels: 166 us -> 182 us
  starting transfers between devices: 14.7 us -> 0 us
  matrix products: 5.79 us -> 0 us
  local copies, waits for them, and re-layouts: 5.16 us -> 1.87 us
  other arithmetic: 2.73 us -> 0 us
    all_to_all x2 -> x0, blocking collectives: 29.7 us -> none  [the longest x1 19.6 us: local(): lax.all_to_all(partial_rows.astype(jnp.bfloat16), ('req', 'ffn'), split_a...]
    all_to_all x1 -> x0, starting transfers between devices: 14.7 us -> none  [local(): lax.all_to_all(own, 'ffn', split_axis=0, concat_axis=0, tiled=True)]
    pallas_call x2 -> x1, Pallas kernels: 58 us -> 69.1 us  [front(): pl.pallas_call(functools.partial(front_body, dims=dims, kn=kn, features=n...]
    dot_general x1 -> x0, matrix products: 5.79 us -> none  [local(): jnp.dot(gather_tokens(attention, 1), out_weight, preferred_element_type=j...]
    pallas_call x1, Pallas kernels: 108 us -> 113 us  [feed_forward(): pl.pallas_call(functools.partial(ffn_body, dims=(hn, ln, cn), kn=kn, rc=r...]
    psum x1 -> x0, blocking collectives: 3.78 us -> none  [local(): squares = lax.psum(jnp.sum(state * state, axis=1), 'kvh')]
  transfers between devices with their start and end apart: 1 -> 0, of which waited for: 0 -> 0; matrix products, arithmetic and copies ran while one was open for 1% -> 0% of each run, Pallas kernels for 0% -> 0%
where the time goes in v2:
time: 187 us; the launch traced here: 184 us
  Pallas kernels  182 us (97%)
  local copies, waits for them, and re-layouts  1.87 us (1%)
    pallas_call x1, Pallas kernels, feed_forward(): pl.pallas_call(functools.partial(ffn_body, dims=(hn, ln, cn), kn=kn, rc=r...  113 us
    pallas_call x1, Pallas kernels, front(): pl.pallas_call(functools.partial(front_body, dims=dims, kn=kn, features=n...  69.1 us

profile of v2, /device:TPU:1, one launch (start us, length us, event | category | flops | bytes accessed | tf_op | source)
XLA Modules:
  0.0 183.8 jit_solution(10971507973437944092)
XLA Ops:
  0.0 69.1 %shard_map.127 = (f32[32,4096]{1,0:T(8,128)}, bf16[32,4096]{1,0:T(8,128)(2,1)}) custom-call(s32[8]{0:T(128)} %len_ref.1, bf16[64,4096]{1,0:T(8,128)(2,1)} %bitcast.8, bf16[64,512]{1,0:T(8,128)(2,1)} %bitcast.9, bf16[64,512]{1,0:T(8,128)(2,1)} %bitcast.10, bf16[4,4096,128]{2,1,0:T(8,128)(2,1)} %bitcast.6, bf16[4,4096,128]{2,1,0:T(8,128)(2,1)} %bitcast.7, ...), custom_call_target="tpu_custom_call" | custom-call | tf_op jit(solution)/shard_map/pallas_call | solution.py:408
  69.1 112.9 %shard_map.128 = f32[32,4096]{1,0:T(8,128)} custom-call(bf16[32,4096]{1,0:T(8,128)(2,1)} %get-tuple-element.7.x_ref, f32[32,4096]{1,0:T(8,128)} %get-tuple-element.8.state_ref, bf16[4096,1792]{1,0:T(8,128)(2,1)} %gate_hbm.1, bf16[4096,1792]{1,0:T(8,128)(2,1)} %up_hbm.1, bf16[1792,4096]{1,0:T(8,128)(2,1)} %down_hbm.1), custom_call_target="tpu_custom_call" | custom-call | tf_op jit(solution)/shard_map/pallas_call | solution.py:730
  181.9 1.9 %copy.15 = f32[32,4096]{1,0:T(8,128)} copy(f32[32,4096]{1,0:T(8,128)} %shard_map.128) | data formatting | bytes 1048576

commit v3 on v0

v3 whole, which is shorter than its diff:
```python
import functools
import math

import jax
import jax.numpy as jnp
from jax import lax
from jax.experimental import pallas as pl
from jax.experimental.pallas import tpu as pltpu
from jax.sharding import PartitionSpec as P

MASKED = -1e30
EPSILON = 1e-05
MESH = pl.DeviceIdType.MESH
ROWS = 16
LAG = 4
BEHIND = 4
PARTS = 8


def split_count(n):
    lo = math.isqrt(n)
    while n % lo:
        lo -= 1
    return n // lo, lo


def lane_block(width, most):
    return max(b for b in range(128, most + 1, 128) if width % b == 0)


def remote(src, dst, send, recv, where):
    return pltpu.make_async_remote_copy(
        src_ref=src, dst_ref=dst, send_sem=send, recv_sem=recv, device_id=where, device_id_type=MESH
    )


class Gather:
    def __init__(self, dims, line, source, target, sems):
        self.dims, self.line, self.source, self.target = dims, line, source, target
        self.z_send, self.z_recv, self.y_send, self.y_recv, self.c_send, self.c_recv, self.own_sem = sems
        req = lax.axis_index("req")
        self.hi, self.lo, self.core = req // dims[1], lax.rem(req, dims[1]), lax.axis_index("ffn")

    def place(self, c, o, g, f=None):
        hn, ln, cn = self.dims
        f = self.core if f is None else f
        return self.target(c, (f * ln + lax.rem(self.lo + ln - g, ln)) * hn + o, f)

    def z_copy(self, c, o, up):
        step = 1 if up else -1
        where = {"req": (self.hi + step) * self.dims[1] + self.lo}
        spot = self.place(c, o, 0)
        return remote(spot, spot, self.z_send.at[c, 0 if up else 1, o], self.z_recv.at[c, o], where)

    def z_own(self, c, up):
        step = 1 if up else -1
        where = {"req": (self.hi + step) * self.dims[1] + self.lo}
        o = self.hi
        return remote(
            self.source(c), self.place(c, o, 0), self.z_send.at[c, 0 if up else 1, o], self.z_recv.at[c, o], where
        )

    def z_far(self, c, e, up):
        o = self.hi
        where = {"req": (o + (e if up else -e)) * self.dims[1] + self.lo}
        at = 0 if up else 1
        return remote(self.source(c), self.place(c, o, 0), self.z_send.at[c, at, e], self.z_recv.at[c, o], where)

    def far(self, body):
        for e in range(1, self.dims[0]):

            @pl.when(self.hi + e < self.dims[0])
            def _(e=e):
                body(e, True)

            @pl.when(self.hi >= e)
            def _(e=e):
                body(e, False)

    def y_copy(self, c, o, d, own=False):
        ln = self.dims[1]
        where = {"req": self.hi * ln + lax.rem(self.lo + d, ln)}
        src = self.source(c) if own else self.place(c, o, 0)
        return remote(src, self.place(c, o, 0), self.y_send.at[c, o, d - 1], self.y_recv.at[c, o, d - 1], where)

    def c_copy(self, c, o, g, d, own=False):
        where = {"ffn": lax.rem(self.core + d, self.dims[2])}
        src = self.source(c) if own else self.place(c, o, g)
        at = o * self.dims[1] + g
        return remote(src, self.place(c, o, g), self.c_send.at[c, at, d - 1], self.c_recv.at[c, at, d - 1], where)

    def own_copy(self, c):
        return pltpu.make_async_copy(self.source(c), self.place(c, self.hi, 0), self.own_sem.at[c])

    def around(self, e, body):
        @pl.when(self.hi >= e)
        def _():
            body(self.hi - e, True)

        @pl.when(self.hi + e < self.dims[0])
        def _():
            body(self.hi + e, False)

    def onward(self, up, body):
        @pl.when(self.hi + 1 < self.dims[0] if up else self.hi > 0)
        def _():
            body()

    def start(self, c):
        hn, ln, cn = self.dims
        if self.line:
            for up in (True, False):
                self.onward(up, lambda up=up: self.z_own(c, up).start())
        else:
            self.far(lambda e, up: self.z_far(c, e, up).start())
        for d in range(1, ln):
            self.y_copy(c, self.hi, d, True).start()
        for d in range(1, cn):
            self.c_copy(c, self.hi, 0, d, True).start()
        self.own_copy(c).start()

    def pass_hi(self, c, reach=None):
        hn, ln, cn = self.dims

        def one(o, up):
            self.z_copy(c, o, up).wait_recv()
            if self.line:
                self.onward(up, lambda: self.z_copy(c, o, up).start())
            for d in range(1, ln):
                self.y_copy(c, o, d).start()
            for d in range(1, cn):
                self.c_copy(c, o, 0, d).start()

        for e in range(1, hn) if reach is None else [reach]:
            self.around(e, one)

    def pass_lo(self, c):
        hn, ln, cn = self.dims

        def one(o, up):
            for g in range(1, ln):
                self.y_copy(c, o, g).wait_recv()
                for d in range(1, cn):
                    self.c_copy(c, o, g, d).start()

        one(self.hi, True)
        for e in range(1, hn):
            self.around(e, one)

    def take(self, c, d, parts=None):
        hn, ln, cn = self.dims
        for g in range(ln) if parts is None else parts:
            for o in range(hn):
                self.c_copy(c, o, g, d).wait_recv()

    def sent(self, c):
        hn, ln, cn = self.dims
        if self.line:
            for up in (True, False):
                self.onward(up, lambda up=up: self.z_own(c, up).wait_send())
            for e in range(1, hn):
                self.around(e, lambda o, up: self.onward(up, lambda: self.z_copy(c, o, up).wait_send()))
        else:
            self.far(lambda e, up: self.z_far(c, e, up).wait_send())
        for o in range(hn):
            for d in range(1, ln):
                self.y_copy(c, o, d).wait_send()
            for g in range(ln):
                for d in range(1, cn):
                    self.c_copy(c, o, g, d).wait_send()


def gather_sems(count, dims):
    hn, ln, cn = dims
    dma = pltpu.SemaphoreType.DMA
    return [
        dma((count, 2, hn)),
        dma((count, hn)),
        dma((count, hn, max(ln - 1, 1))),
        dma((count, hn, max(ln - 1, 1))),
        dma((count, hn * ln, max(cn - 1, 1))),
        dma((count, hn * ln, max(cn - 1, 1))),
        dma((count,)),
    ]


def layer_body(
    len_ref, q_ref, tk_ref, tv_ref, k_hbm, v_hbm, par_ref, res_hbm, gain_ref, wo_hbm, gate_hbm, up_hbm, down_hbm, out_ref,
    gath, state, normed, half_got, pack, blocks_got, cross_got, squares, squares_got,
    rbuf, part, got, act, dbuf, got_core, mid, own_mid, got_lo, low, own_low, got_hi,
    k_sem, v_sem, wo_sem, res_sem, w_sem, wd_sem,
    a0, a1, a2, a3, a4, a5, a6, d0, d1, d2, d3, d4, d5, d6,
    x_send, x_recv, b_send, b_recv, f_send, f_recv, s_send, s_recv,
    p_send, p_recv, a_send, a_recv, c_send, c_recv, l_send, l_recv, h_send, h_recv,
    *, dims, kn, heads, hc, fw,
):
    hn, ln, cn = dims
    n = hn * ln * cn
    req = lax.axis_index("req")
    hi, lo, core, k = req // ln, lax.rem(req, ln), lax.axis_index("ffn"), lax.axis_index("kvh")
    span, size = k_hbm.shape[1:]
    nodes = q_ref.shape[0]
    group = q_ref.shape[1] // (heads * size)
    wide = group * size
    rows = group * nodes
    mine = nodes // cn
    part_rows = group * mine
    fb = pack.shape[1]
    per = n // kn
    width = normed.shape[1]
    features = width * kn
    factor = size**-0.5 * math.log2(math.e)
    chunk = math.gcd(span, 1024)
    hidden_width = act.shape[2]
    hs = hidden_width // hc
    fs = width // fw
    to_hi = lambda d: {"req": lax.rem(hi + d, hn) * ln + lo}
    to_lo = lambda d: {"req": hi * ln + lax.rem(lo + d, ln)}
    to_core = lambda d: {"ffn": lax.rem(core + d, cn)}
    to_kvh = lambda d: {"kvh": lax.rem(k + d, kn)}
    flat = [(e, g, d) for e in range(hn) for g in range(ln) for d in range(cn)]

    def plane(e, g, d):
        return {"req": lax.rem(hi + e, hn) * ln + lax.rem(lo + g, ln), "ffn": lax.rem(core + d, cn)}

    barrier = pltpu.get_barrier_semaphore()
    peers = [plane(*t) for t in flat[1:]] + [to_kvh(d) for d in range(1, kn)]
    for where in peers:
        pl.semaphore_signal(barrier, inc=1, device_id=where, device_id_type=MESH)

    def attention_phase(kbuf, vbuf, wo, sbuf, tree_mask, half_own, attn, proj):
        k_copy = lambda h: pltpu.make_async_copy(k_hbm.at[h], kbuf.at[h], k_sem.at[h])
        v_copy = lambda h: pltpu.make_async_copy(v_hbm.at[h], vbuf.at[h], v_sem.at[h])
        wo_copy = pltpu.make_async_copy(wo_hbm, wo, wo_sem)
        for h in range(heads):
            k_copy(h).start()
            v_copy(h).start()
        wo_copy.start()
        pltpu.make_async_copy(res_hbm, state, res_sem).start()
        live = jnp.clip(len_ref[lax.axis_index("req")] - core * span, 0, span)

        up = lax.broadcasted_iota(jnp.int32, (nodes, nodes), 0)
        across = lax.broadcasted_iota(jnp.int32, (nodes, nodes), 1)
        eye = jnp.where(up == across, 1.0, 0.0).astype(jnp.bfloat16)
        link = jnp.where(up == par_ref[...], 1.0, 0.0).astype(jnp.bfloat16)
        over = lax.dot_general(link, eye, (((0,), (0,)), ((), ())), preferred_element_type=jnp.float32)
        reach = jnp.minimum(over + jnp.where(up == across, 1.0, 0.0), 1.0)
        for _ in range((nodes - 1).bit_length()):
            half = reach.astype(jnp.bfloat16)
            reach = jnp.minimum(jnp.dot(half, half, preferred_element_type=jnp.float32), 1.0)
        reach = reach * jnp.where(core == 0, 1.0, 0.0)
        tree_mask[...] = jnp.concatenate(
            [reach[f * mine : (f + 1) * mine] for f in range(cn) for _ in range(group)], axis=0
        )
        def head_cols(h):
            return pl.ds(pl.multiple_of(h * size, size), size)

        def queries_of(h):
            return jnp.concatenate(
                [
                    q_ref[f * mine : (f + 1) * mine, pl.ds(pl.multiple_of((h * group + g) * size, size), size)]
                    for f in range(cn)
                    for g in range(group)
                ],
                axis=0,
            )

        def tree_scores(h):
            s = lax.dot_general(
                queries_of(h), tk_ref[:, head_cols(h)], (((1,), (1,)), ((), ())), preferred_element_type=jnp.float32
            )
            return jnp.where(tree_mask[...] > 0.5, s, MASKED)

        def score(h):
            k_copy(h).wait()
            q = queries_of(h)
            first = kbuf[h, pl.ds(0, 16), :].astype(jnp.float32)[0:1]
            top = jnp.max(tree_scores(h), axis=1, keepdims=True)
            for c in range(span // chunk):
                spot = c * chunk + lax.broadcasted_iota(jnp.int32, (chunk, size), 0)
                keys = jnp.where(spot < live, kbuf[h, pl.ds(c * chunk, chunk), :].astype(jnp.float32), first)
                s = lax.dot_general(
                    q, keys.astype(jnp.bfloat16), (((1,), (1,)), ((), ())), preferred_element_type=jnp.float32
                )
                sbuf[:, pl.ds(c * chunk, chunk)] = s
                top = jnp.maximum(top, jnp.max(s, axis=1, keepdims=True))
            half_own[h, :, pl.ds(size, size)] = jnp.broadcast_to(top, (rows, size))

        def weigh(h):
            v_copy(h).wait()
            top = half_own[h, :, pl.ds(size, 1)]
            usable = tree_mask[...] > 0.5
            w = jnp.where(usable, jnp.exp2((tree_scores(h) - top) * factor), 0.0).astype(jnp.bfloat16)
            ones = jnp.ones((nodes, size), jnp.bfloat16)
            total = jnp.dot(
                w, jnp.concatenate([tv_ref[:, head_cols(h)], ones], axis=1), preferred_element_type=jnp.float32
            )
            for c in range(span // chunk):
                spot = c * chunk + lax.broadcasted_iota(jnp.int32, (chunk, size), 0)
                usable = spot < live
                values = jnp.where(usable, vbuf[h, pl.ds(c * chunk, chunk), :].astype(jnp.float32), 0.0)
                count = jnp.where(usable, 1.0, 0.0)
                both = jnp.concatenate([values.astype(jnp.bfloat16), count.astype(jnp.bfloat16)], axis=1)
                w = jnp.exp2((sbuf[:, pl.ds(c * chunk, chunk)] - top) * factor).astype(jnp.bfloat16)
                total = total + jnp.dot(w, both, preferred_element_type=jnp.float32)
            seen = jnp.where((live > 0) | (core == 0), 1.0, 0.0)
            top = jnp.where(seen > 0.5, top * factor, MASKED)
            lane = lax.broadcasted_iota(jnp.int32, (rows, size), 1)
            half_own[h, :, pl.ds(0, size)] = total[:, :size]
            half_own[h, :, pl.ds(size, size)] = jnp.where(lane < size // 2, total[:, size:], top)
            for d in range(1, cn):
                half_copy(h, d).start()
        def part_of(f):
            return pl.ds(pl.multiple_of(f * part_rows, part_rows), part_rows)

        def half_copy(h, d):
            src = half_own.at[h, part_of(lax.rem(core + d, cn)), :]
            return remote(src, half_got.at[h, d - 1], x_send.at[h, d - 1], x_recv.at[h, d - 1], to_core(d))

        def merge(h):
            for d in range(1, cn):
                half_copy(h, d).wait_recv()
            pieces = [half_own[h, part_of(core), :]] + [half_got[h, d] for d in range(cn - 1)]
            tops = [p[:, size + size // 2 : size + size // 2 + 1] for p in pieces]
            best = functools.reduce(jnp.maximum, tops)
            above, below = 0.0, 0.0
            for p, t in zip(pieces, tops):
                scale = jnp.exp2(t - best)
                above = above + p[:, :size] * scale
                below = below + p[:, size : size + 1] * scale
            result = (above / below).astype(jnp.bfloat16)
            for g in range(group):
                attn[h, :, pl.ds(g * size, size)] = result[g * mine : (g + 1) * mine]
        gather = Gather(
            dims,
            True,
            lambda h: attn.at[h],
            lambda h, b, f: gath.at[
                pl.ds(pl.multiple_of(b * mine, mine), mine), pl.ds(pl.multiple_of(h * wide, wide), wide)
            ],
            (a0, a1, a2, a3, a4, a5, a6),
        )

        def finish(h):
            for d in range(1, cn):
                gather.take(h, d)
            gather.own_copy(h).wait()

        def project(h):
            cols = pl.ds(pl.multiple_of(h * wide, wide), wide)
            piece = jnp.dot(gath[:, cols], wo[cols, :], preferred_element_type=jnp.float32)

            @pl.when(h == 0)
            def _():
                proj[...] = piece

            @pl.when(h > 0)
            def _():
                proj[...] = proj[...] + piece

        def guarded(h, *stages):
            @pl.when((h >= 0) & (h < heads))
            def _():
                for stage in stages:
                    with jax.named_scope(stage.__name__):
                        stage(h)

        def step(i, carry):
            guarded(i, score)

            @pl.when(i == 0)
            def _():
                with jax.named_scope("barrier_wait"):
                    pl.semaphore_wait(barrier, len(peers))

            guarded(i - 1, merge, gather.start)
            for e in range(1, hn):

                def pass_hi(h, e=e):
                    gather.pass_hi(h, e)

                guarded(i - 1 - e, pass_hi)
            guarded(i, weigh)
            guarded(i - 1 - hn, gather.pass_lo)

            @pl.when(i == 2)
            def _():
                wo_copy.wait()

            guarded(i - 2 - hn, finish, project)
            return carry

        lax.fori_loop(0, heads + 2 + hn, step, 0)
        pack[...] = proj[...].astype(jnp.bfloat16)

        def sent(h, carry):
            gather.sent(h)
            for d in range(1, cn):
                half_copy(h, d).wait_send()
            return carry

        lax.fori_loop(0, heads, sent, 0)

    def forward_phase(wgu, wd):
        wd_slots, r_slots, m_slots, t_slots = wd.shape[0], rbuf.shape[0], own_mid.shape[0], dbuf.shape[0] - fs
        chunks = mine // ROWS
        items = chunks * cn
        steps = items * hs
        loads = (chunks - 1 + cn) * fs
        tokens = n // cn * ROWS
        keep = tokens // kn
        half_rows = hn * ROWS

        def weight_copies(h):
            cols = pl.ds(pl.multiple_of(h * hc, hc), hc)
            return (
                pltpu.make_async_copy(gate_hbm.at[:, cols], wgu.at[h, :, pl.ds(0, hc)], w_sem.at[0, h]),
                pltpu.make_async_copy(up_hbm.at[:, cols], wgu.at[h, :, pl.ds(hc, hc)], w_sem.at[1, h]),
            )

        def down_copy(j):
            slot = lax.rem(j, wd_slots)
            cols = pl.ds(pl.multiple_of(lax.rem(j, fs) * fw, fw), fw)
            return pltpu.make_async_copy(down_hbm.at[:, cols], wd.at[slot], wd_sem.at[slot])

        for h in range(hs):
            for copy in weight_copies(h):
                copy.start()
        for j in range(min(wd_slots, loads)):
            down_copy(j).start()
        def rows_at(e, g, d):
            b = (lax.rem(core + d, cn) * ln + lax.rem(lo + g, ln)) * hn + lax.rem(hi + e, hn)
            return pl.ds(pl.multiple_of(b * mine, mine), mine)

        def block_copy(t):
            e, g, d = flat[t]
            return remote(pack.at[rows_at(e, g, d), :], blocks_got.at[t], b_send.at[t], b_recv.at[t], plane(e, g, d))

        far_first = sorted(range(1, n), key=lambda t: -min(flat[t][0], hn - flat[t][0]))
        for t in far_first:
            block_copy(t).start()
        blocks_got[0] = pack[rows_at(0, 0, 0), :]

        def origin(b):
            f, r = lax.rem(b, cn), lax.div(b, cn)
            h, l = lax.div(r, ln), lax.rem(r, ln)
            return (lax.rem(hi + hn - h, hn) * ln + lax.rem(lo + ln - l, ln)) * cn + lax.rem(core + cn - f, cn)

        def arrived(t):
            @pl.when(t > 0)
            def _():
                remote(
                    pack.at[pl.ds(0, mine), :], blocks_got.at[t], b_send.at[t], b_recv.at[t], to_core(1)
                ).wait_recv()

        def cross_copy(d, t):
            return remote(blocks_got.at[t], cross_got.at[d - 1, t], f_send.at[d - 1, t], f_recv.at[d - 1, t], to_kvh(d))

        for d in range(1, kn):

            def forward(j, carry, d=d):
                t = origin(lax.rem(k + d, kn) * per + j)
                arrived(t)
                cross_copy(d, t).start()
                return carry

            with jax.named_scope("forward"):
                lax.fori_loop(0, per, forward, 0)

        def collect(j, square):
            t = origin(k * per + j)
            arrived(t)
            total = blocks_got[t].astype(jnp.float32)
            for d in range(1, kn):
                cross_copy(d, t).wait_recv()
                total = total + cross_got[d - 1, t].astype(jnp.float32)
            cols = pl.ds(pl.multiple_of(j * fb, fb), fb)
            total = total + state[:, cols]
            state[:, cols] = total
            return square + jnp.sum(total * total, axis=1, keepdims=True)

        pltpu.make_async_copy(res_hbm, state, res_sem).wait()
        with jax.named_scope("collect"):
            square = lax.fori_loop(0, per, collect, jnp.zeros((mine, 1), jnp.float32))
        squares[...] = jnp.broadcast_to(square, squares.shape)

        def square_copy(d):
            return remote(squares, squares_got.at[d - 1], s_send.at[d - 1], s_recv.at[d - 1], to_kvh(d))

        for d in range(1, kn):
            square_copy(d).start()
        for d in range(1, kn):
            square_copy(d).wait_recv()
            square = square + squares_got[d - 1, :, pl.ds(0, 1)]
        scale = lax.rsqrt(square / features + EPSILON)

        def norm(j, carry):
            cols = pl.ds(pl.multiple_of(j * fb, fb), fb)
            normed[:, cols] = (state[:, cols] * scale * gain_ref[:, cols]).astype(jnp.bfloat16)
            return carry

        lax.fori_loop(0, per, norm, 0)
        gather = Gather(
            dims,
            False,
            lambda c: normed.at[pl.ds(pl.multiple_of(c * ROWS, ROWS), ROWS), :],
            lambda c, b, f: gath.at[pl.ds(pl.multiple_of(c * (n * ROWS) + b * ROWS, ROWS), ROWS), :],
            (d0, d1, d2, d3, d4, d5, d6),
        )

        def mine_of(item):
            return core == lax.rem(item, cn)

        def on_owner(item, stage):
            @pl.when(mine_of(item))
            def _():
                stage(lax.div(item, cn))

        def ready(item, own=True, parts=None):
            c = lax.div(item, cn)
            if own:

                @pl.when(mine_of(item))
                def _():
                    gather.own_copy(c).wait()

            for d in range(1, cn):

                @pl.when(lax.rem(core + cn - d, cn) == lax.rem(item, cn))
                def _(d=d):
                    gather.take(c, d, parts)

        item_rows = lambda item: pl.ds(pl.multiple_of(item * tokens, tokens), tokens)
        mine_rows = pl.ds(pl.multiple_of(k * keep, keep), keep)

        def part_copy(s, d):
            return remote(part.at[lax.rem(s, PARTS), d - 1], got.at[s, d - 1], p_send.at[s, d - 1], p_recv.at[s, d - 1], to_kvh(d))

        def hidden(s):
            item, h = lax.div(s, hs), lax.rem(s, hs)
            slot = lax.rem(s, r_slots)
            rbuf[slot] = jnp.dot(gath[item_rows(item), :], wgu[h], preferred_element_type=jnp.float32)
            for d in range(1, kn):

                @pl.when(s >= PARTS)
                def _(d=d):
                    part_copy(s - PARTS, d).wait_send()

                theirs = pl.ds(pl.multiple_of(lax.rem(k + d, kn) * keep, keep), keep)
                part[lax.rem(s, PARTS), d - 1] = rbuf[slot, theirs, :].astype(jnp.bfloat16)
                part_copy(s, d).start()

        def act_copy(s, d):
            item, h = lax.div(s, hs), lax.rem(s, hs)
            spot = act.at[item, mine_rows, pl.ds(pl.multiple_of(h * hc, hc), hc)]
            return remote(spot, spot, a_send.at[s, d - 1], a_recv.at[s, d - 1], to_kvh(d))

        def activate(s):
            item, h = lax.div(s, hs), lax.rem(s, hs)
            slot = lax.rem(s, r_slots)
            for d in range(1, kn):
                part_copy(s, d).wait_recv()
            gate = rbuf[slot, mine_rows, pl.ds(0, hc)]
            up = rbuf[slot, mine_rows, pl.ds(hc, hc)]
            for d in range(kn - 1):
                gate = gate + got[s, d, :, pl.ds(0, hc)].astype(jnp.float32)
                up = up + got[s, d, :, pl.ds(hc, hc)].astype(jnp.float32)
            value = (gate / (1.0 + jnp.exp(-gate)) * up).astype(jnp.bfloat16)
            act[item, mine_rows, pl.ds(pl.multiple_of(h * hc, hc), hc)] = value
            for d in range(1, kn):
                act_copy(s, d).start()

        def activated(item):
            def one(h, carry):
                for d in range(1, kn):
                    act_copy(item * hs + h, d).wait_recv()
                return carry

            lax.fori_loop(0, hs, one, 0)

        def kept(item, i):
            return lax.div(item, cn) * fs + i

        def down_slot(item, i):
            j = kept(item, i)
            return jnp.where(mine_of(item), lax.rem(j, fs), fs + lax.rem(j, t_slots))

        def down_send(item, i, d):
            j = kept(item, i)
            return remote(
                dbuf.at[fs + lax.rem(j, t_slots)], got_core.at[j, d - 1], c_send.at[d - 1, j], c_recv.at[j, d - 1], to_core(d)
            )

        def each_core(item, body):
            for d in range(1, cn):

                @pl.when(lax.rem(core + d, cn) == lax.rem(item, cn))
                def _(d=d):
                    body(d)

        def multiply(load, members, i):
            down_copy(load).wait()
            for item in members:

                @pl.when(kept(item, i) >= t_slots)
                def _(item=item):
                    each_core(item, lambda d: down_send(item, i - t_slots, d).wait_send())

                dbuf[down_slot(item, i)] = jnp.dot(
                    act[item], wd[lax.rem(load, wd_slots)], preferred_element_type=jnp.float32
                )
                each_core(item, lambda d: down_send(item, i, d).start())

            @pl.when(load + wd_slots < loads)
            def _():
                down_copy(load + wd_slots).start()

        def mid_send(item, i, d):
            j = kept(item, i)
            return remote(mid.at[j, d - 1], got_lo.at[j, d - 1], l_send.at[j, d - 1], l_recv.at[j, d - 1], to_lo(d))

        def low_send(item, i, d):
            j = kept(item, i)
            return remote(low.at[j, d - 1], got_hi.at[j, d - 1], h_send.at[j, d - 1], h_recv.at[j, d - 1], to_hi(d))

        def add_core(item, i):
            j = kept(item, i)
            slot = lax.rem(j, fs)
            for d in range(1, cn):
                down_send(item, i, d).wait_recv()

            def total(b):
                at = pl.ds(pl.multiple_of(b * half_rows, half_rows), half_rows)
                result = dbuf[slot, at, :]
                for d in range(cn - 1):
                    result = result + got_core[j, d, at, :]
                return result

            for d in range(1, ln):
                mid[j, d - 1] = total(lax.rem(lo + d, ln)).astype(jnp.bfloat16)
                mid_send(item, i, d).start()
            own_mid[lax.rem(j, m_slots)] = total(lo)

        def add_lo(item, i):
            j = kept(item, i)
            slot = lax.rem(j, m_slots)
            for d in range(1, ln):
                mid_send(item, i, d).wait_recv()

            def total(h):
                at = pl.ds(pl.multiple_of(h * ROWS, ROWS), ROWS)
                result = own_mid[slot, at, :]
                for d in range(ln - 1):
                    result = result + got_lo[j, d, at, :].astype(jnp.float32)
                return result

            for d in range(1, hn):
                low[j, d - 1] = total(lax.rem(hi + d, hn)).astype(jnp.bfloat16)
                low_send(item, i, d).start()
            own_low[j] = total(hi)

        def add_hi(item, i):
            j = kept(item, i)
            c = lax.div(item, cn)
            for d in range(1, hn):
                low_send(item, i, d).wait_recv()
            result = own_low[j]
            for d in range(hn - 1):
                result = result + got_hi[j, d].astype(jnp.float32)
            at = (pl.ds(pl.multiple_of(c * ROWS, ROWS), ROWS), pl.ds(pl.multiple_of(i * fw, fw), fw))
            out_ref[at] = state[at] + result

        def within(i, stage, *args):
            @pl.when((i >= 0) & (i < fs))
            def _():
                with jax.named_scope(stage.__name__.strip('<>')):
                    stage(*args, i)

        def down_all(c, i):
            within(i, lambda i: multiply(c * fs + i, [c * cn + f for f in range(cn)], i))

        def down_one(item, i):
            within(i, lambda i: multiply((chunks - 1 + lax.rem(item, cn)) * fs + i, [item], i))

        def owned(item, i, stage):
            @pl.when(mine_of(item))
            def _():
                within(i, stage, item)

        def stretch(at, first, per_step, stage):
            @pl.when((at >= first) & (at - first < -(-fs // per_step)))
            def _():
                def one(i, carry):
                    stage((at - first) * per_step + i)
                    return carry

                lax.fori_loop(0, per_step, one, 0)

        on_owner(0, gather.start)
        with jax.named_scope("first_hi"):
            on_owner(0, gather.pass_hi)
        with jax.named_scope("first_lo"):
            on_owner(0, gather.pass_lo)
        with jax.named_scope("first_ready"):
            ready(0, False, range(1))
            for f in range(1, cn):
                on_owner(f, gather.start)
            ready(0, True, range(1, ln))

        def step(s, carry):
            item, h = lax.div(s, hs), lax.rem(s, hs)
            fresh = item + 1

            @pl.when(s < hs)
            def _():
                for copy in weight_copies(h):
                    copy.wait()

            @pl.when(s < steps)
            def _():
                with jax.named_scope("hidden"):
                    hidden(s)

            @pl.when((s >= BEHIND) & (s < steps + BEHIND))
            def _():
                with jax.named_scope("activate"):
                    activate(s - BEHIND)

            turn = lax.rem(s, hs * cn)
            c = lax.div(s, hs * cn)
            front_core = core == 0
            mark = lambda at, stage, to, when: pl.when((turn == at) & when & (to < chunks))(lambda: stage(to))
            mark(3, gather.pass_hi, c, (c == 0) & ~front_core)
            mark(5, gather.pass_lo, c, (c == 0) & ~front_core)
            total = hs * cn
            mark(total - 13, gather.start, c + 1, front_core)
            mark(total - 8, gather.start, c + 1, ~front_core)
            mark(total - 6, gather.pass_hi, c + 1, front_core)
            mark(total - 4, gather.pass_lo, c + 1, front_core)
            mark(total - 4, gather.pass_hi, c + 1, ~front_core)
            mark(total - 2, gather.pass_lo, c + 1, ~front_core)

            @pl.when((h == hs - 1) & (fresh < items))
            def _():
                with jax.named_scope("ready"):
                    ready(fresh)

            offset = BEHIND + 2
            begun = lax.div(s - offset, total) - 1
            since = lax.rem(s - offset, total)

            @pl.when((s >= total + offset) & (begun < chunks - 1))
            def _():
                @pl.when(since == 0)
                def _():
                    for f in range(cn):
                        with jax.named_scope("activated"):
                            activated(begun * cn + f)

                stretch(since, 0, 2, lambda i: down_all(begun, i))
                stretch(since, 2, 2, lambda i: within(i, add_core, begun * cn + core))
                stretch(since, 5, 2, lambda i: within(i, add_lo, begun * cn + core))

            for f in range(cn - 1):
                item = (chunks - 1) * cn + f
                opened = s - (hs * (item + 1) + BEHIND + 1)

                @pl.when(opened == 0)
                def _(item=item):
                    with jax.named_scope("activated"):
                        activated(item)

                stretch(opened, 0, 4, lambda i, item=item: down_one(item, i))
                stretch(opened, 1, 4, lambda i, item=item: owned(item, i, add_core))
                stretch(opened, 3, 4, lambda i, item=item: owned(item, i, add_lo))

            return carry

        lax.fori_loop(0, steps + BEHIND, step, 0)
        with jax.named_scope("activated_last"):
            activated(items - 1)

        def last(i, carry):
            down_one(items - 1, i)
            owned(items - 1, i - LAG, add_core)
            owned(items - 1, i - 2 * LAG - 1, add_lo)
            return carry

        lax.fori_loop(0, 2 * fs + LAG, last, 0)
        for c in range(chunks):

            def end(i, carry, c=c):
                within(i, add_hi, c * cn + core)
                return carry

            lax.fori_loop(0, fs, end, 0)

        def sent_rows(c, carry):
            gather.sent(c)
            return carry

        with jax.named_scope('sent_rows'):
            lax.fori_loop(0, chunks, sent_rows, 0)

        def sent_steps(s, carry):
            for d in range(1, kn):

                @pl.when(s >= steps - PARTS)
                def _(d=d):
                    part_copy(s, d).wait_send()

                act_copy(s, d).wait_send()
            return carry

        with jax.named_scope('sent_steps'):
            lax.fori_loop(0, steps, sent_steps, 0)

        for item in range(items):
            for i in range(fs):
                if item // cn * fs + i + t_slots >= chunks * fs:
                    each_core(item, lambda d, item=item, i=i: down_send(item, i, d).wait_send())

        def sent_pieces(j, carry):
            item, i = lax.div(j, fs) * cn + core, lax.rem(j, fs)
            for d in range(1, ln):
                mid_send(item, i, d).wait_send()
            for d in range(1, hn):
                low_send(item, i, d).wait_send()
            return carry

        with jax.named_scope('sent_pieces'):
            lax.fori_loop(0, chunks * fs, sent_pieces, 0)
        for t in range(1, n):
            block_copy(t).wait_send()
        for d in range(1, kn):

            def cross_sent(j, carry, d=d):
                cross_copy(d, origin(lax.rem(k + d, kn) * per + j)).wait_send()
                return carry

            lax.fori_loop(0, per, cross_sent, 0)
            square_copy(d).wait_send()

    b16 = jnp.bfloat16
    pl.run_scoped(
        attention_phase,
        pltpu.VMEM((heads, span, size), b16),
        pltpu.VMEM((heads, span, size), b16),
        pltpu.VMEM(wo_hbm.shape, b16),
        pltpu.VMEM((rows, span), jnp.float32),
        pltpu.VMEM((rows, nodes), jnp.float32),
        pltpu.VMEM((heads, rows, 2 * size), jnp.float32),
        pltpu.VMEM((heads, mine, wide), b16),
        pltpu.VMEM((n * mine, fb), jnp.float32),
    )
    pl.run_scoped(
        forward_phase,
        pltpu.VMEM((hs, width, 2 * hc), b16),
        pltpu.VMEM((3, hidden_width, fw), b16),
    )


def layer(
    queries, tree_keys, tree_values, keys, values, lengths, parents, residual, out_weight, norm_gain, gate_weight, up_weight,
    down_weight,
):
    dims = (*split_count(lax.axis_size("req")), lax.axis_size("ffn"))
    hn, ln, cn = dims
    kn = lax.axis_size("kvh")
    n = math.prod(dims)
    heads, span, size = keys.shape
    nodes, width = queries.shape
    wide = width // heads
    rows = wide // size * nodes
    mine, cols = residual.shape
    fb = out_weight.shape[1]
    hidden = gate_weight.shape[1]
    hc = lane_block(hidden, 256)
    fw = lane_block(cols, max(128, cols // 8))
    chunks = mine // ROWS
    items = chunks * cn
    tokens = n // cn * ROWS
    keep = tokens // kn
    steps = items * (hidden // hc)
    kept = chunks * (cols // fw)
    vmem = pl.BlockSpec(memory_space=pltpu.VMEM)
    hbm = pl.BlockSpec(memory_space=pl.ANY)
    f32, b16 = jnp.float32, jnp.bfloat16
    dma = pltpu.SemaphoreType.DMA
    return pl.pallas_call(
        functools.partial(layer_body, dims=dims, kn=kn, heads=heads, hc=hc, fw=fw),
        out_shape=jax.ShapeDtypeStruct(residual.shape, f32),
        in_specs=[
            pl.BlockSpec(memory_space=pltpu.SMEM), vmem, vmem, vmem, hbm, hbm, vmem, hbm, vmem, hbm, hbm, hbm, hbm,
        ],
        out_specs=vmem,
        scratch_shapes=[
            pltpu.VMEM((n * mine, width), b16),
            pltpu.VMEM((mine, cols), f32),
            pltpu.VMEM((mine, cols), b16),
            pltpu.VMEM((heads, cn - 1, rows // cn, 2 * size), f32),
            pltpu.VMEM((n * mine, fb), b16),
            pltpu.VMEM((n, mine, fb), b16),
            pltpu.VMEM((kn - 1, n, mine, fb), b16),
            pltpu.VMEM((mine, 128), f32),
            pltpu.VMEM((kn - 1, mine, 128), f32),
            pltpu.VMEM((BEHIND + 1, tokens, 2 * hc), f32),
            pltpu.VMEM((PARTS, kn - 1, keep, 2 * hc), b16),
            pltpu.VMEM((steps, kn - 1, keep, 2 * hc), b16),
            pltpu.VMEM((items, tokens, hidden), b16),
            pltpu.VMEM((cols // fw + 3, tokens, fw), f32),
            pltpu.VMEM((kept, cn - 1, tokens, fw), f32),
            pltpu.VMEM((kept, ln - 1, hn * ROWS, fw), b16),
            pltpu.VMEM((cols // fw, hn * ROWS, fw), f32),
            pltpu.VMEM((kept, ln - 1, hn * ROWS, fw), b16),
            pltpu.VMEM((kept, hn - 1, ROWS, fw), b16),
            pltpu.VMEM((kept, ROWS, fw), f32),
            pltpu.VMEM((kept, hn - 1, ROWS, fw), b16),
            dma((heads,)),
            dma((heads,)),
            dma,
            dma,
            dma((2, hidden // hc)),
            dma((3,)),
            *gather_sems(heads, dims),
            *gather_sems(chunks, dims),
            dma((heads, cn - 1)),
            dma((heads, cn - 1)),
            dma((n,)),
            dma((n,)),
            dma((kn - 1, n)),
            dma((kn - 1, n)),
            dma((kn - 1,)),
            dma((kn - 1,)),
            dma((steps, kn - 1)),
            dma((steps, kn - 1)),
            dma((steps, kn - 1)),
            dma((steps, kn - 1)),
            dma((cn - 1, kept)),
            dma((kept, cn - 1)),
            dma((kept, ln - 1)),
            dma((kept, ln - 1)),
            dma((kept, hn - 1)),
            dma((kept, hn - 1)),
        ],
        compiler_params=pltpu.CompilerParams(collective_id=1, has_side_effects=True, vmem_limit_bytes=63 * 1024 * 1024),
    )(
        lengths, queries, tree_keys, tree_values, keys, values, parents, residual, norm_gain[None, :], out_weight,
        gate_weight, up_weight, down_weight,
    )


def local(
    queries, tree_keys, tree_token_values, cache_keys, cached_value_rows, lengths, parents, residual, out_weight, norm_gain,
    gate_weight, up_weight, down_weight,
):
    return layer(
        queries[0], tree_keys[0], tree_token_values[0], cache_keys[0], cached_value_rows[0], lengths, parents, residual,
        out_weight, norm_gain, gate_weight, up_weight, down_weight,
    )


def solution(mesh):
    in_specs = (
        P("req", None, "kvh"),
        P("req", None, "kvh"),
        P("req", None, "kvh"),
        P("req", "kvh", "ffn", None),
        P("req", "kvh", "ffn", None),
        P(),
        P("req", None),
        P(("req", "ffn"), "kvh"),
        P("kvh", ("req", "ffn")),
        P("kvh"),
        P("kvh", ("req", "ffn")),
        P("kvh", ("req", "ffn")),
        P(("req", "ffn"), "kvh"),
    )
    out_specs = P(("req", "ffn"), "kvh")
    return jax.shard_map(local, mesh=mesh, in_specs=in_specs, out_specs=out_specs, check_vma=False)
```

time: 318 us -> 174 us (0.55)
  matrix products: 46.3 us -> 0 us
  blocking collectives: 30.8 us -> 0 us
  Pallas kernels: 196 us -> 172 us
  starting transfers between devices: 22.4 us -> 0 us
  waiting for transfers between devices: 7.69 us -> 0 us
  local copies, waits for them, and re-layouts: 8.6 us -> 1.87 us
    dot_general x4 -> x0, matrix products: 46.3 us -> none  [the longest x1 14.5 us: local(): up_part = jnp.dot(block_rows, up_weight, preferred_element_type=jnp.float32)]
    all_to_all x1 -> x0, blocking collectives: 24.8 us -> none  [local(): lax.all_to_all(partial_rows.astype(jnp.bfloat16), ('req', 'ffn'), split_a...]
    pallas_call x5 -> x1, Pallas kernels: 196 us -> 172 us  [layer(): pl.pallas_call(functools.partial(layer_body, dims=dims, kn=kn, heads=head...]
    all_to_all x2 -> x0, starting transfers between devices: 22.4 us -> none  [the longest x1 18.9 us: local(): lax.all_to_all(own, 'ffn', split_axis=0, concat_axis=0, tiled=True)]
    all_to_all x2 -> x0, waiting for transfers between devices: 7.69 us -> none  [the longest x1 7.68 us: local(): lax.all_to_all(regrouped, 'kvh', split_axis=1, concat_axis=0, tiled=True)]
    psum x1 -> x0, blocking collectives: 3.96 us -> none  [local(): squares = lax.psum(jnp.sum(state * state, axis=1), 'kvh')]
  transfers between devices with their start and end apart: 2 -> 0, of which waited for: 1 -> 0; matrix products, arithmetic and copies ran while one was open for 0% -> 0% of each run, Pallas kernels for 0% -> 0%
where the time goes in v3:
time: 174 us
  Pallas kernels  172 us (99%)
  local copies, waits for them, and re-layouts  1.87 us (1%)
    pallas_call x1, Pallas kernels, layer(): pl.pallas_call(functools.partial(layer_body, dims=dims, kn=kn, heads=head...  172 us

profile of v3, /device:TPU:1, one launch (start us, length us, event | category | flops | bytes accessed | tf_op | source)
XLA Modules:
  0.0 173.7 jit_solution(15546445035277450546)
XLA Ops:
  0.0 171.8 %shard_map.127 = f32[32,4096]{1,0:T(8,128)} custom-call(s32[8]{0:T(128)} %len_ref.1, bf16[64,4096]{1,0:T(8,128)(2,1)} %bitcast.8, bf16[64,512]{1,0:T(8,128)(2,1)} %bitcast.9, bf16[64,512]{1,0:T(8,128)(2,1)} %bitcast.10, bf16[4,4096,128]{2,1,0:T(8,128)(2,1)} %bitcast.6, bf16[4,4096,128]{2,1,0:T(8,128)(2,1)} %bitcast.7, s32[1,64]{1,0:T(1,128)} %par_ref.1, ...), custom_call_target="tpu_custom_call" | custom-call | tf_op jit(solution)/shard_map/pallas_call | solution.py:890
  171.8 1.9 %copy.15 = f32[32,4096]{1,0:T(8,128)} copy(f32[32,4096]{1,0:T(8,128)} %shard_map.127) | data formatting | bytes 1048576

commit v4 on v3

--- a/solution.py
+++ b/solution.py
@@ -44,62 +44,77 @@
     def place(self, c, o, g, f=None):
         hn, ln, cn = self.dims
         f = self.core if f is None else f
-        return self.target(c, (f * ln + lax.rem(self.lo + ln - g, ln)) * hn + o, f)
+        return self.target(c, (f * ln + lax.rem(self.lo + ln - g, ln)) * hn + o, 1)
 
     def z_copy(self, c, o, up):
         step = 1 if up else -1
         where = {"req": (self.hi + step) * self.dims[1] + self.lo}
         spot = self.place(c, o, 0)
-        return remote(spot, spot, self.z_send.at[c, 0 if up else 1, o], self.z_recv.at[c, o], where)
+        return remote(spot, spot, self.z_send.at[c], self.z_recv.at[c, o], where)
 
     def z_own(self, c, up):
         step = 1 if up else -1
         where = {"req": (self.hi + step) * self.dims[1] + self.lo}
         o = self.hi
         return remote(
-            self.source(c), self.place(c, o, 0), self.z_send.at[c, 0 if up else 1, o], self.z_recv.at[c, o], where
+            self.source(c), self.place(c, o, 0), self.z_send.at[c], self.z_recv.at[c, o], where
         )
 
     def z_far(self, c, e, up):
         o = self.hi
         where = {"req": (o + (e if up else -e)) * self.dims[1] + self.lo}
-        at = 0 if up else 1
-        return remote(self.source(c), self.place(c, o, 0), self.z_send.at[c, at, e], self.z_recv.at[c, o], where)
+        return remote(self.source(c), self.place(c, o, 0), self.z_send.at[c], self.z_recv.at[c, o], where)
 
     def far(self, body):
         for e in range(1, self.dims[0]):
 
-            @pl.when(self.hi + e < self.dims[0])
-            def _(e=e):
-                body(e, True)
-
-            @pl.when(self.hi >= e)
-            def _(e=e):
-                body(e, False)
+            def above(e=e):
+                @pl.when(self.hi + e < self.dims[0])
+                def _():
+                    body(e, True)
+
+            def below(e=e):
+                @pl.when(self.hi >= e)
+                def _():
+                    body(e, False)
+
+            self.end_first(below, above)
 
     def y_copy(self, c, o, d, own=False):
         ln = self.dims[1]
         where = {"req": self.hi * ln + lax.rem(self.lo + d, ln)}
         src = self.source(c) if own else self.place(c, o, 0)
-        return remote(src, self.place(c, o, 0), self.y_send.at[c, o, d - 1], self.y_recv.at[c, o, d - 1], where)
+        return remote(src, self.place(c, o, 0), self.y_send.at[c], self.y_recv.at[c, o, d - 1], where)
 
     def c_copy(self, c, o, g, d, own=False):
         where = {"ffn": lax.rem(self.core + d, self.dims[2])}
         src = self.source(c) if own else self.place(c, o, g)
-        at = o * self.dims[1] + g
-        return remote(src, self.place(c, o, g), self.c_send.at[c, at, d - 1], self.c_recv.at[c, at, d - 1], where)
+        return remote(src, self.place(c, o, g), self.c_send.at[c], self.c_recv.at[c, g, d - 1], where)
 
     def own_copy(self, c):
         return pltpu.make_async_copy(self.source(c), self.place(c, self.hi, 0), self.own_sem.at[c])
 
+    def end_first(self, down, up):
+        low = 2 * self.hi < self.dims[0]
+        for first in (True, False):
+
+            @pl.when(low if first else ~low)
+            def _(first=first):
+                for stage in (down, up) if first else (up, down):
+                    stage()
+
     def around(self, e, body):
-        @pl.when(self.hi >= e)
-        def _():
-            body(self.hi - e, True)
-
-        @pl.when(self.hi + e < self.dims[0])
-        def _():
-            body(self.hi + e, False)
+        def below():
+            @pl.when(self.hi >= e)
+            def _():
+                body(self.hi - e, True)
+
+        def above():
+            @pl.when(self.hi + e < self.dims[0])
+            def _():
+                body(self.hi + e, False)
+
+        self.end_first(above, below)
 
     def onward(self, up, body):
         @pl.when(self.hi + 1 < self.dims[0] if up else self.hi > 0)
@@ -107,12 +122,17 @@
             body()
 
     def start(self, c):
-        hn, ln, cn = self.dims
+        self.start_hi(c)
+        self.start_rest(c)
+
+    def start_hi(self, c):
         if self.line:
-            for up in (True, False):
-                self.onward(up, lambda up=up: self.z_own(c, up).start())
+            self.end_first(*(lambda up=up: self.onward(up, lambda: self.z_own(c, up).start()) for up in (False, True)))
         else:
             self.far(lambda e, up: self.z_far(c, e, up).start())
+
+    def start_rest(self, c):
+        hn, ln, cn = self.dims
         for d in range(1, ln):
             self.y_copy(c, self.hi, d, True).start()
         for d in range(1, cn):
@@ -149,48 +169,51 @@
 
     def take(self, c, d, parts=None):
         hn, ln, cn = self.dims
+        where = {"ffn": lax.rem(self.core + d, cn)}
         for g in range(ln) if parts is None else parts:
-            for o in range(hn):
-                self.c_copy(c, o, g, d).wait_recv()
+            f, b = lax.rem(self.core + cn - d, cn), lax.rem(self.lo + ln - g, ln)
+            spot = self.target(c, (f * ln + b) * hn, hn)
+            remote(spot, spot, self.c_send.at[c], self.c_recv.at[c, g, d - 1], where).wait_recv()
 
     def sent(self, c):
         hn, ln, cn = self.dims
+        where = {"ffn": lax.rem(self.core + 1, cn)}
+
+        def gone(sem, count):
+            spot = self.target(c, 0, count)
+            remote(spot, spot, sem.at[c], self.c_recv.at[c, 0, 0], where).wait_send()
+
         if self.line:
-            for up in (True, False):
-                self.onward(up, lambda up=up: self.z_own(c, up).wait_send())
-            for e in range(1, hn):
-                self.around(e, lambda o, up: self.onward(up, lambda: self.z_copy(c, o, up).wait_send()))
+            inner = (self.hi > 0) & (self.hi + 1 < hn)
+            pl.when(inner)(lambda: gone(self.z_send, hn + 1))
+            pl.when(~inner)(lambda: gone(self.z_send, 1))
         else:
-            self.far(lambda e, up: self.z_far(c, e, up).wait_send())
-        for o in range(hn):
-            for d in range(1, ln):
-                self.y_copy(c, o, d).wait_send()
-            for g in range(ln):
-                for d in range(1, cn):
-                    self.c_copy(c, o, g, d).wait_send()
+            gone(self.z_send, hn - 1)
+        gone(self.y_send, hn * (ln - 1))
+        gone(self.c_send, hn * ln * (cn - 1))
 
 
 def gather_sems(count, dims):
     hn, ln, cn = dims
     dma = pltpu.SemaphoreType.DMA
     return [
-        dma((count, 2, hn)),
+        dma((count,)),
         dma((count, hn)),
-        dma((count, hn, max(ln - 1, 1))),
-        dma((count, hn, max(ln - 1, 1))),
-        dma((count, hn * ln, max(cn - 1, 1))),
-        dma((count, hn * ln, max(cn - 1, 1))),
+        dma((count,)),
+        dma((count, hn, ln - 1)),
+        dma((count,)),
+        dma((count, ln, cn - 1)),
         dma((count,)),
     ]
 
 
 def layer_body(
     len_ref, q_ref, tk_ref, tv_ref, k_hbm, v_hbm, par_ref, res_hbm, gain_ref, wo_hbm, gate_hbm, up_hbm, down_hbm, out_ref,
-    gath, state, normed, half_got, pack, blocks_got, cross_got, squares, squares_got,
+    gath, state, normed, half_got, pack, pack_got, red, blocks_got, cross_got, squares, squares_got, line_own, lines, factor_of,
     rbuf, part, got, act, dbuf, got_core, mid, own_mid, got_lo, low, own_low, got_hi,
     k_sem, v_sem, wo_sem, res_sem, w_sem, wd_sem,
     a0, a1, a2, a3, a4, a5, a6, d0, d1, d2, d3, d4, d5, d6,
-    x_send, x_recv, b_send, b_recv, f_send, f_recv, s_send, s_recv,
+    x_send, x_recv, y_send, y_recv, b_send, b_recv, f_send, f_recv, s_send, s_recv, r_send, r_recv, told,
     p_send, p_recv, a_send, a_recv, c_send, c_recv, l_send, l_recv, h_send, h_recv,
     *, dims, kn, heads, hc, fw,
 ):
@@ -205,7 +228,7 @@
     rows = group * nodes
     mine = nodes // cn
     part_rows = group * mine
-    fb = pack.shape[1]
+    fb = red.shape[2]
     per = n // kn
     width = normed.shape[1]
     features = width * kn
@@ -223,6 +246,7 @@
     def plane(e, g, d):
         return {"req": lax.rem(hi + e, hn) * ln + lax.rem(lo + g, ln), "ffn": lax.rem(core + d, cn)}
 
+    own_block = (core * ln + lo) * hn + hi
     barrier = pltpu.get_barrier_semaphore()
     peers = [plane(*t) for t in flat[1:]] + [to_kvh(d) for d in range(1, kn)]
     for where in peers:
@@ -315,7 +339,7 @@
 
         def half_copy(h, d):
             src = half_own.at[h, part_of(lax.rem(core + d, cn)), :]
-            return remote(src, half_got.at[h, d - 1], x_send.at[h, d - 1], x_recv.at[h, d - 1], to_core(d))
+            return remote(src, half_got.at[h, d - 1], x_send.at[d - 1], x_recv.at[h, d - 1], to_core(d))
 
         def merge(h):
             for d in range(1, cn):
@@ -335,8 +359,8 @@
             dims,
             True,
             lambda h: attn.at[h],
-            lambda h, b, f: gath.at[
-                pl.ds(pl.multiple_of(b * mine, mine), mine), pl.ds(pl.multiple_of(h * wide, wide), wide)
+            lambda h, b, count: gath.at[
+                pl.ds(pl.multiple_of(b * mine, mine), count * mine), pl.ds(pl.multiple_of(h * wide, wide), wide)
             ],
             (a0, a1, a2, a3, a4, a5, a6),
         )
@@ -391,22 +415,68 @@
             return carry
 
         lax.fori_loop(0, heads + 2 + hn, step, 0)
-        pack[...] = proj[...].astype(jnp.bfloat16)
-
         def sent(h, carry):
             gather.sent(h)
-            for d in range(1, cn):
-                half_copy(h, d).wait_send()
             return carry
 
         lax.fori_loop(0, heads, sent, 0)
+        for d in range(1, cn):
+            spot = half_got.at[:, d - 1]
+            remote(spot, spot, x_send.at[d - 1], x_recv.at[0, d - 1], to_core(d)).wait_send()
+
+        def rows_of(b):
+            return pl.ds(pl.multiple_of(b * mine, mine), mine)
+
+        def halve_copy(m, d):
+            return remote(pack.at[d - 1, m], pack_got.at[d - 1, m], y_send.at[d - 1], y_recv.at[d - 1, m], to_kvh(d))
+
+        order = sorted(range(hn), key=lambda e: -min(e, hn - e))
+
+        def in_order(i):
+            e, q = lax.div(i, per // hn), lax.rem(i, per // hn)
+            shift = functools.reduce(lambda x, at: jnp.where(e == at, order[at], x), range(hn), 0)
+            return q * hn + lax.rem(hi + shift, hn)
+
+        def halve(i, carry):
+            m = in_order(i)
+            for d in range(1, kn):
+                pack[d - 1, m] = proj[rows_of(lax.rem(k + d, kn) * per + m), :].astype(jnp.bfloat16)
+                halve_copy(m, d).start()
+            return carry
+
+        lax.fori_loop(0, per, halve, 0)
+
+        def deliver(i, carry):
+            m = in_order(i)
+            b = k * per + m
+            total = proj[rows_of(b), :]
+            for d in range(1, kn):
+                halve_copy(m, d).wait_recv()
+                total = total + pack_got[d - 1, m].astype(jnp.float32)
+            red[m] = total.astype(jnp.bfloat16)
+            own = req * cn + core
+
+            @pl.when(b == own_block)
+            def _():
+                blocks_got[own] = red[m]
+
+            @pl.when(b != own_block)
+            def _():
+                f, r = lax.div(b, ln * hn), lax.rem(b, ln * hn)
+                where = {"req": lax.rem(r, hn) * ln + lax.div(r, hn), "ffn": f}
+                remote(red.at[m], blocks_got.at[own], b_send, b_recv.at[own], where).start()
+
+            return carry
+
+        with jax.named_scope("deliver"):
+            lax.fori_loop(0, per, deliver, 0)
 
     def forward_phase(wgu, wd):
         wd_slots, r_slots, m_slots, t_slots = wd.shape[0], rbuf.shape[0], own_mid.shape[0], dbuf.shape[0] - fs
         chunks = mine // ROWS
         items = chunks * cn
         steps = items * hs
-        loads = (chunks - 1 + cn) * fs
+        loads = (chunks - 2 + cn) * fs + wd_slots
         tokens = n // cn * ROWS
         keep = tokens // kn
         half_rows = hn * ROWS
@@ -414,8 +484,8 @@
         def weight_copies(h):
             cols = pl.ds(pl.multiple_of(h * hc, hc), hc)
             return (
-                pltpu.make_async_copy(gate_hbm.at[:, cols], wgu.at[h, :, pl.ds(0, hc)], w_sem.at[0, h]),
-                pltpu.make_async_copy(up_hbm.at[:, cols], wgu.at[h, :, pl.ds(hc, hc)], w_sem.at[1, h]),
+                pltpu.make_async_copy(gate_hbm.at[:, cols], wgu.at[h, :, pl.ds(0, hc)], w_sem.at[h]),
+                pltpu.make_async_copy(up_hbm.at[:, cols], wgu.at[h, :, pl.ds(hc, hc)], w_sem.at[h]),
             )
 
         def down_copy(j):
@@ -428,60 +498,54 @@
                 copy.start()
         for j in range(min(wd_slots, loads)):
             down_copy(j).start()
-        def rows_at(e, g, d):
-            b = (lax.rem(core + d, cn) * ln + lax.rem(lo + g, ln)) * hn + lax.rem(hi + e, hn)
-            return pl.ds(pl.multiple_of(b * mine, mine), mine)
-
-        def block_copy(t):
-            e, g, d = flat[t]
-            return remote(pack.at[rows_at(e, g, d), :], blocks_got.at[t], b_send.at[t], b_recv.at[t], plane(e, g, d))
-
-        far_first = sorted(range(1, n), key=lambda t: -min(flat[t][0], hn - flat[t][0]))
-        for t in far_first:
-            block_copy(t).start()
-        blocks_got[0] = pack[rows_at(0, 0, 0), :]
-
-        def origin(b):
-            f, r = lax.rem(b, cn), lax.div(b, cn)
-            h, l = lax.div(r, ln), lax.rem(r, ln)
-            return (lax.rem(hi + hn - h, hn) * ln + lax.rem(lo + ln - l, ln)) * cn + lax.rem(core + cn - f, cn)
-
-        def arrived(t):
-            @pl.when(t > 0)
-            def _():
-                remote(
-                    pack.at[pl.ds(0, mine), :], blocks_got.at[t], b_send.at[t], b_recv.at[t], to_core(1)
-                ).wait_recv()
-
-        def cross_copy(d, t):
-            return remote(blocks_got.at[t], cross_got.at[d - 1, t], f_send.at[d - 1, t], f_recv.at[d - 1, t], to_kvh(d))
-
-        for d in range(1, kn):
-
-            def forward(j, carry, d=d):
-                t = origin(lax.rem(k + d, kn) * per + j)
-                arrived(t)
-                cross_copy(d, t).start()
-                return carry
-
-            with jax.named_scope("forward"):
+        kept_here = lax.div(own_block, per) == k
+        keeper = lax.div(own_block, per)
+
+        def cross_copy(j, d):
+            b = lax.rem(k + d, kn) * per + j
+            return remote(blocks_got.at[b], cross_got.at[j], f_send.at[d - 1], f_recv.at[j], to_kvh(d))
+
+        def arrived(b):
+            @pl.when(b != req * cn + core)
+            def _():
+                remote(red.at[0], blocks_got.at[b], b_send, b_recv.at[b], to_core(1)).wait_recv()
+
+        @pl.when(kept_here)
+        def _():
+            for d in range(1, kn):
+
+                def forward(j, carry, d=d):
+                    arrived(lax.rem(k + d, kn) * per + j)
+                    cross_copy(j, d).start()
+                    return carry
+
                 lax.fori_loop(0, per, forward, 0)
 
         def collect(j, square):
-            t = origin(k * per + j)
-            arrived(t)
-            total = blocks_got[t].astype(jnp.float32)
-            for d in range(1, kn):
-                cross_copy(d, t).wait_recv()
-                total = total + cross_got[d - 1, t].astype(jnp.float32)
             cols = pl.ds(pl.multiple_of(j * fb, fb), fb)
-            total = total + state[:, cols]
-            state[:, cols] = total
+
+            @pl.when(kept_here)
+            def _():
+                arrived(k * per + j)
+                state[:, cols] = state[:, cols] + blocks_got[k * per + j].astype(jnp.float32)
+
+            @pl.when(~kept_here)
+            def _():
+                cross_copy(j, 1).wait_recv()
+                state[:, cols] = state[:, cols] + cross_got[j].astype(jnp.float32)
+
+            total = state[:, cols]
+            normed[:, cols] = (total * gain_ref[:, cols]).astype(jnp.bfloat16)
             return square + jnp.sum(total * total, axis=1, keepdims=True)
 
         pltpu.make_async_copy(res_hbm, state, res_sem).wait()
         with jax.named_scope("collect"):
             square = lax.fori_loop(0, per, collect, jnp.zeros((mine, 1), jnp.float32))
+        @pl.when(kept_here)
+        def _():
+            for d in range(1, kn):
+                pl.semaphore_signal(told, inc=1, device_id=to_kvh(d), device_id_type=MESH)
+
         squares[...] = jnp.broadcast_to(square, squares.shape)
 
         def square_copy(d):
@@ -489,22 +553,45 @@
 
         for d in range(1, kn):
             square_copy(d).start()
-        for d in range(1, kn):
-            square_copy(d).wait_recv()
-            square = square + squares_got[d - 1, :, pl.ds(0, 1)]
-        scale = lax.rsqrt(square / features + EPSILON)
-
-        def norm(j, carry):
-            cols = pl.ds(pl.multiple_of(j * fb, fb), fb)
-            normed[:, cols] = (state[:, cols] * scale * gain_ref[:, cols]).astype(jnp.bfloat16)
-            return carry
-
-        lax.fori_loop(0, per, norm, 0)
+
+        @pl.when(~kept_here)
+        def _():
+            pl.semaphore_wait(told, 1)
+
+        def share_squares():
+            total = squares[...]
+            for d in range(1, kn):
+                square_copy(d).wait_recv()
+                total = total + squares_got[d - 1]
+            same = lax.broadcasted_iota(jnp.int32, total.shape, 0) == lax.broadcasted_iota(jnp.int32, total.shape, 1)
+            line = jnp.sum(jnp.where(same, total, 0.0), axis=0, keepdims=True)
+            line_own[...] = jnp.broadcast_to(line, line_own.shape)
+            lines[own_block] = line_own[...]
+            for t in range(1, n):
+                line_copy(t).start()
+
+        def line_copy(t):
+            return remote(line_own, lines.at[own_block], r_send, r_recv, plane(*flat[t]))
+
+        def all_lines():
+            return remote(lines.at[pl.ds(0, n - 1)], lines.at[pl.ds(0, n - 1)], r_send, r_recv, plane(*flat[1]))
+
+        def factors():
+            all_lines().wait_recv()
+            for item in range(items):
+                for m in range(keep // ROWS):
+                    b = (item % cn) * (ln * hn) + k * (keep // ROWS) + m
+                    wide_line = jnp.broadcast_to(lines[b, pl.ds(0, 1), :], (ROWS, 128))
+                    spot = lax.broadcasted_iota(jnp.int32, (ROWS, 128), 0) + (item // cn) * ROWS
+                    picked = jnp.where(lax.broadcasted_iota(jnp.int32, (ROWS, 128), 1) == spot, wide_line, 0.0)
+                    total = jnp.sum(picked, axis=1, keepdims=True)
+                    column = lax.rsqrt(total / features + EPSILON)
+                    factor_of[item, pl.ds(m * ROWS, ROWS), :] = jnp.broadcast_to(column, (ROWS, 128))
         gather = Gather(
             dims,
             False,
             lambda c: normed.at[pl.ds(pl.multiple_of(c * ROWS, ROWS), ROWS), :],
-            lambda c, b, f: gath.at[pl.ds(pl.multiple_of(c * (n * ROWS) + b * ROWS, ROWS), ROWS), :],
+            lambda c, b, count: gath.at[pl.ds(pl.multiple_of(c * (n * ROWS) + b * ROWS, ROWS), count * ROWS), :],
             (d0, d1, d2, d3, d4, d5, d6),
         )
 
@@ -534,7 +621,10 @@
         mine_rows = pl.ds(pl.multiple_of(k * keep, keep), keep)
 
         def part_copy(s, d):
-            return remote(part.at[lax.rem(s, PARTS), d - 1], got.at[s, d - 1], p_send.at[s, d - 1], p_recv.at[s, d - 1], to_kvh(d))
+            return remote(
+                part.at[lax.rem(s, PARTS), d - 1], got.at[s, d - 1], p_send.at[lax.rem(s, PARTS), d - 1],
+                p_recv.at[lax.rem(s, 3 * BEHIND), d - 1], to_kvh(d),
+            )
 
         def hidden(s):
             item, h = lax.div(s, hs), lax.rem(s, hs)
@@ -553,7 +643,7 @@
         def act_copy(s, d):
             item, h = lax.div(s, hs), lax.rem(s, hs)
             spot = act.at[item, mine_rows, pl.ds(pl.multiple_of(h * hc, hc), hc)]
-            return remote(spot, spot, a_send.at[s, d - 1], a_recv.at[s, d - 1], to_kvh(d))
+            return remote(spot, spot, a_send.at[d - 1], a_recv.at[item, d - 1], to_kvh(d))
 
         def activate(s):
             item, h = lax.div(s, hs), lax.rem(s, hs)
@@ -565,18 +655,18 @@
             for d in range(kn - 1):
                 gate = gate + got[s, d, :, pl.ds(0, hc)].astype(jnp.float32)
                 up = up + got[s, d, :, pl.ds(hc, hc)].astype(jnp.float32)
+            scale = factor_of[item, :, pl.ds(0, 1)]
+            gate, up = gate * scale, up * scale
             value = (gate / (1.0 + jnp.exp(-gate)) * up).astype(jnp.bfloat16)
             act[item, mine_rows, pl.ds(pl.multiple_of(h * hc, hc), hc)] = value
             for d in range(1, kn):
                 act_copy(s, d).start()
 
         def activated(item):
-            def one(h, carry):
-                for d in range(1, kn):
-                    act_copy(item * hs + h, d).wait_recv()
-                return carry
-
-            lax.fori_loop(0, hs, one, 0)
+            for d in range(1, kn):
+                theirs = pl.ds(pl.multiple_of(lax.rem(k + kn - d, kn) * keep, keep), keep)
+                spot = act.at[item, theirs, :]
+                remote(spot, spot, a_send.at[d - 1], a_recv.at[item, d - 1], to_kvh(d)).wait_recv()
 
         def kept(item, i):
             return lax.div(item, cn) * fs + i
@@ -588,7 +678,8 @@
         def down_send(item, i, d):
             j = kept(item, i)
             return remote(
-                dbuf.at[fs + lax.rem(j, t_slots)], got_core.at[j, d - 1], c_send.at[d - 1, j], c_recv.at[j, d - 1], to_core(d)
+                dbuf.at[fs + lax.rem(j, t_slots)], got_core.at[j, d - 1], c_send.at[d - 1, lax.rem(j, t_slots)],
+                c_recv.at[j, d - 1], to_core(d),
             )
 
         def each_core(item, body):
@@ -598,30 +689,47 @@
                 def _(d=d):
                     body(d)
 
-        def multiply(load, members, i):
-            down_copy(load).wait()
-            for item in members:
+        spare = min(fs - wd_slots, hs)
+
+        def spare_copy(i):
+            cols = pl.ds((wd_slots + i) * fw, fw)
+            room = wgu.at[i, pl.ds(0, hidden_width), pl.ds(0, fw)]
+            return pltpu.make_async_copy(down_hbm.at[:, cols], room, w_sem.at[i])
+
+        def settle(members, i, result):
+            for at, item in enumerate(members):
 
                 @pl.when(kept(item, i) >= t_slots)
                 def _(item=item):
                     each_core(item, lambda d: down_send(item, i - t_slots, d).wait_send())
 
-                dbuf[down_slot(item, i)] = jnp.dot(
-                    act[item], wd[lax.rem(load, wd_slots)], preferred_element_type=jnp.float32
-                )
-                each_core(item, lambda d: down_send(item, i, d).start())
+                dbuf[down_slot(item, i)] = result[at * tokens : (at + 1) * tokens]
+                each_core(item, lambda d, item=item: down_send(item, i, d).start())
+
+        def multiply(load, members, i):
+            down_copy(load).wait()
+            first = members[0]
+            rows = act[pl.ds(first, len(members))].reshape(len(members) * tokens, hidden_width)
+            settle(members, i, jnp.dot(rows, wd[lax.rem(load, wd_slots)], preferred_element_type=jnp.float32))
 
             @pl.when(load + wd_slots < loads)
             def _():
                 down_copy(load + wd_slots).start()
+
+        def multiply_spare(item, i):
+            pltpu.make_async_copy(
+                down_hbm.at[:, pl.ds(0, fw)], wgu.at[0, pl.ds(0, hidden_width), pl.ds(0, fw)], w_sem.at[i - wd_slots]
+            ).wait()
+            weight = wgu[i - wd_slots, pl.ds(0, hidden_width), pl.ds(0, fw)]
+            settle([item], i, jnp.dot(act[item], weight, preferred_element_type=jnp.float32))
 
         def mid_send(item, i, d):
             j = kept(item, i)
-            return remote(mid.at[j, d - 1], got_lo.at[j, d - 1], l_send.at[j, d - 1], l_recv.at[j, d - 1], to_lo(d))
+            return remote(mid.at[j, d - 1], got_lo.at[j, d - 1], l_send.at[d - 1], l_recv.at[j, d - 1], to_lo(d))
 
         def low_send(item, i, d):
             j = kept(item, i)
-            return remote(low.at[j, d - 1], got_hi.at[j, d - 1], h_send.at[j, d - 1], h_recv.at[j, d - 1], to_hi(d))
+            return remote(low.at[j, d - 1], got_hi.at[j, d - 1], h_send, h_recv.at[j], to_hi(d))
 
         def add_core(item, i):
             j = kept(item, i)
@@ -662,8 +770,7 @@
         def add_hi(item, i):
             j = kept(item, i)
             c = lax.div(item, cn)
-            for d in range(1, hn):
-                low_send(item, i, d).wait_recv()
+            remote(got_hi.at[j], got_hi.at[j], h_send, h_recv.at[j], to_hi(1)).wait_recv()
             result = own_low[j]
             for d in range(hn - 1):
                 result = result + got_hi[j, d].astype(jnp.float32)
@@ -676,11 +783,22 @@
                 with jax.named_scope(stage.__name__.strip('<>')):
                     stage(*args, i)
 
+        quick = -(-fs // 2)
+
         def down_all(c, i):
             within(i, lambda i: multiply(c * fs + i, [c * cn + f for f in range(cn)], i))
 
         def down_one(item, i):
-            within(i, lambda i: multiply((chunks - 1 + lax.rem(item, cn)) * fs + i, [item], i))
+            within(i, lambda i: multiply((chunks - 1 + item % cn) * fs + i, [item], i))
+
+        def down_last(i):
+            @pl.when(i < wd_slots)
+            def _():
+                multiply(loads - wd_slots + i, [items - 1], i)
+
+            @pl.when((i >= wd_slots) & (i < fs))
+            def _():
+                multiply_spare(items - 1, i)
 
         def owned(item, i, stage):
             @pl.when(mine_of(item))
@@ -697,15 +815,21 @@
                 lax.fori_loop(0, per_step, one, 0)
 
         on_owner(0, gather.start)
+        pl.when((core > 0) & kept_here)(lambda: gather.start(0))
         with jax.named_scope("first_hi"):
             on_owner(0, gather.pass_hi)
+            pl.when((core > 0) & kept_here)(lambda: gather.pass_hi(0))
+        with jax.named_scope("share"):
+            share_squares()
         with jax.named_scope("first_lo"):
             on_owner(0, gather.pass_lo)
         with jax.named_scope("first_ready"):
             ready(0, False, range(1))
             for f in range(1, cn):
-                on_owner(f, gather.start)
+                pl.when((core == f) & ~kept_here)(lambda: gather.start_hi(0))
             ready(0, True, range(1, ln))
+            for f in range(1, cn):
+                pl.when((core == f) & ~kept_here)(lambda: gather.start_rest(0))
 
         def step(s, carry):
             item, h = lax.div(s, hs), lax.rem(s, hs)
@@ -713,8 +837,7 @@
 
             @pl.when(s < hs)
             def _():
-                for copy in weight_copies(h):
-                    copy.wait()
+                pltpu.make_async_copy(gate_hbm.at[:, pl.ds(0, 2 * hc)], wgu.at[h], w_sem.at[h]).wait()
 
             @pl.when(s < steps)
             def _():
@@ -723,6 +846,11 @@
 
             @pl.when((s >= BEHIND) & (s < steps + BEHIND))
             def _():
+                @pl.when(s == BEHIND)
+                def _():
+                    with jax.named_scope("factors"):
+                        factors()
+
                 with jax.named_scope("activate"):
                     activate(s - BEHIND)
 
@@ -730,8 +858,9 @@
             c = lax.div(s, hs * cn)
             front_core = core == 0
             mark = lambda at, stage, to, when: pl.when((turn == at) & when & (to < chunks))(lambda: stage(to))
-            mark(3, gather.pass_hi, c, (c == 0) & ~front_core)
-            mark(5, gather.pass_lo, c, (c == 0) & ~front_core)
+            mark(1, gather.pass_lo, c, (c == 0) & ~front_core & kept_here)
+            mark(3, gather.pass_hi, c, (c == 0) & ~front_core & ~kept_here)
+            mark(5, gather.pass_lo, c, (c == 0) & ~front_core & ~kept_here)
             total = hs * cn
             mark(total - 13, gather.start, c + 1, front_core)
             mark(total - 8, gather.start, c + 1, ~front_core)
@@ -745,7 +874,7 @@
                 with jax.named_scope("ready"):
                     ready(fresh)
 
-            offset = BEHIND + 2
+            offset = BEHIND + 3
             begun = lax.div(s - offset, total) - 1
             since = lax.rem(s - offset, total)
 
@@ -763,16 +892,23 @@
 
             for f in range(cn - 1):
                 item = (chunks - 1) * cn + f
-                opened = s - (hs * (item + 1) + BEHIND + 1)
+                opened = s - (hs * (item + 1) + BEHIND + 2)
 
                 @pl.when(opened == 0)
                 def _(item=item):
                     with jax.named_scope("activated"):
                         activated(item)
 
-                stretch(opened, 0, 4, lambda i, item=item: down_one(item, i))
-                stretch(opened, 1, 4, lambda i, item=item: owned(item, i, add_core))
-                stretch(opened, 3, 4, lambda i, item=item: owned(item, i, add_lo))
+                stretch(opened, 1, quick, lambda i, item=item: owned(item, i, add_core))
+                stretch(opened, 0, quick, lambda i, item=item: down_one(item, i))
+
+                if f == cn - 2:
+
+                    @pl.when(opened == 1)
+                    def _():
+                        for i in range(spare):
+                            spare_copy(i).start()
+
 
             return carry
 
@@ -781,8 +917,10 @@
             activated(items - 1)
 
         def last(i, carry):
-            down_one(items - 1, i)
+            down_last(i)
             owned(items - 1, i - LAG, add_core)
+            for f in range(cn - 1):
+                owned((chunks - 1) * cn + f, i - LAG, add_lo)
             owned(items - 1, i - 2 * LAG - 1, add_lo)
             return carry
 
@@ -809,9 +947,11 @@
                 def _(d=d):
                     part_copy(s, d).wait_send()
 
-                act_copy(s, d).wait_send()
             return carry
 
+        for d in range(1, kn):
+            spot = act.at[:, mine_rows, :]
+            remote(spot, spot, a_send.at[d - 1], a_recv.at[0, d - 1], to_kvh(d)).wait_send()
         with jax.named_scope('sent_steps'):
             lax.fori_loop(0, steps, sent_steps, 0)
 
@@ -820,25 +960,27 @@
                 if item // cn * fs + i + t_slots >= chunks * fs:
                     each_core(item, lambda d, item=item, i=i: down_send(item, i, d).wait_send())
 
-        def sent_pieces(j, carry):
-            item, i = lax.div(j, fs) * cn + core, lax.rem(j, fs)
-            for d in range(1, ln):
-                mid_send(item, i, d).wait_send()
-            for d in range(1, hn):
-                low_send(item, i, d).wait_send()
-            return carry
-
-        with jax.named_scope('sent_pieces'):
-            lax.fori_loop(0, chunks * fs, sent_pieces, 0)
-        for t in range(1, n):
-            block_copy(t).wait_send()
+        for d in range(1, ln):
+            spot = mid.at[:, d - 1]
+            remote(spot, spot, l_send.at[d - 1], l_recv.at[0, d - 1], to_lo(d)).wait_send()
+        remote(low, low, h_send, h_recv.at[0], to_hi(1)).wait_send()
         for d in range(1, kn):
-
-            def cross_sent(j, carry, d=d):
-                cross_copy(d, origin(lax.rem(k + d, kn) * per + j)).wait_send()
-                return carry
-
-            lax.fori_loop(0, per, cross_sent, 0)
+            spot = pack.at[d - 1]
+            remote(spot, spot, y_send.at[d - 1], y_recv.at[d - 1, 0], to_kvh(d)).wait_send()
+        gone = lambda count: remote(
+            red.at[pl.ds(0, count)], red.at[pl.ds(0, count)], b_send, b_recv.at[0], to_core(1)
+        ).wait_send()
+        pl.when(kept_here)(lambda: gone(per - 1))
+        pl.when(~kept_here)(lambda: gone(per))
+        all_lines().wait_send()
+
+        @pl.when(kept_here)
+        def _():
+            for d in range(1, kn):
+                spot = blocks_got.at[pl.ds(0, per)]
+                remote(spot, spot, f_send.at[d - 1], f_recv.at[0], to_kvh(d)).wait_send()
+
+        for d in range(1, kn):
             square_copy(d).wait_send()
 
     b16 = jnp.bfloat16
@@ -899,11 +1041,16 @@
             pltpu.VMEM((mine, cols), f32),
             pltpu.VMEM((mine, cols), b16),
             pltpu.VMEM((heads, cn - 1, rows // cn, 2 * size), f32),
-            pltpu.VMEM((n * mine, fb), b16),
+            pltpu.VMEM((kn - 1, n // kn, mine, fb), b16),
+            pltpu.VMEM((kn - 1, n // kn, mine, fb), b16),
+            pltpu.VMEM((n // kn, mine, fb), b16),
             pltpu.VMEM((n, mine, fb), b16),
-            pltpu.VMEM((kn - 1, n, mine, fb), b16),
+            pltpu.VMEM((n // kn, mine, fb), b16),
             pltpu.VMEM((mine, 128), f32),
             pltpu.VMEM((kn - 1, mine, 128), f32),
+            pltpu.VMEM((8, 128), f32),
+            pltpu.VMEM((n, 8, 128), f32),
+            pltpu.VMEM((items, keep, 128), f32),
             pltpu.VMEM((BEHIND + 1, tokens, 2 * hc), f32),
             pltpu.VMEM((PARTS, kn - 1, keep, 2 * hc), b16),
             pltpu.VMEM((steps, kn - 1, keep, 2 * hc), b16),
@@ -920,28 +1067,33 @@
             dma((heads,)),
             dma,
             dma,
-            dma((2, hidden // hc)),
+            dma((hidden // hc,)),
             dma((3,)),
             *gather_sems(heads, dims),
             *gather_sems(chunks, dims),
+            dma((cn - 1,)),
             dma((heads, cn - 1)),
-            dma((heads, cn - 1)),
+            dma((kn - 1,)),
+            dma((kn - 1, n // kn)),
+            dma,
             dma((n,)),
-            dma((n,)),
-            dma((kn - 1, n)),
-            dma((kn - 1, n)),
+            dma((kn - 1,)),
+            dma((n // kn,)),
             dma((kn - 1,)),
             dma((kn - 1,)),
-            dma((steps, kn - 1)),
-            dma((steps, kn - 1)),
-            dma((steps, kn - 1)),
-            dma((steps, kn - 1)),
-            dma((cn - 1, kept)),
+            dma,
+            dma,
+            pltpu.SemaphoreType.REGULAR,
+            dma((PARTS, kn - 1)),
+            dma((3 * BEHIND, kn - 1)),
+            dma((kn - 1,)),
+            dma((items, kn - 1)),
+            dma((cn - 1, 3)),
             dma((kept, cn - 1)),
+            dma((ln - 1,)),
             dma((kept, ln - 1)),
-            dma((kept, ln - 1)),
-            dma((kept, hn - 1)),
-            dma((kept, hn - 1)),
+            dma,
+            dma((kept,)),
         ],
         compiler_params=pltpu.CompilerParams(collective_id=1, has_side_effects=True, vmem_limit_bytes=63 * 1024 * 1024),
     )(

time: 174 us -> 154 us (0.89)
  Pallas kernels: 172 us -> 151 us
    pallas_call x1, Pallas kernels: 172 us -> 151 us  [layer(): pl.pallas_call(functools.partial(layer_body, dims=dims, kn=kn, heads=head...]
where the time goes in v4:
time: 154 us; the launch traced here: 153 us
  Pallas kernels  151 us (98%)
  local copies, waits for them, and re-layouts  1.87 us (1%)
    pallas_call x1, Pallas kernels, layer(): pl.pallas_call(functools.partial(layer_body, dims=dims, kn=kn, heads=head...  151 us

profile of v4, /device:TPU:1, one launch (start us, length us, event | category | flops | bytes accessed | tf_op | source)
XLA Modules:
  0.0 153.0 jit_solution(16944448782090847947)
XLA Ops:
  0.0 151.1 %shard_map.127 = f32[32,4096]{1,0:T(8,128)} custom-call(s32[8]{0:T(128)} %len_ref.1, bf16[64,4096]{1,0:T(8,128)(2,1)} %bitcast.8, bf16[64,512]{1,0:T(8,128)(2,1)} %bitcast.9, bf16[64,512]{1,0:T(8,128)(2,1)} %bitcast.10, bf16[4,4096,128]{2,1,0:T(8,128)(2,1)} %bitcast.6, bf16[4,4096,128]{2,1,0:T(8,128)(2,1)} %bitcast.7, s32[1,64]{1,0:T(1,128)} %par_ref.1, ...), custom_call_target="tpu_custom_call" | custom-call | tf_op jit(solution)/shard_map/pallas_call | solution.py:1032
  151.1 1.9 %copy.15 = f32[32,4096]{1,0:T(8,128)} copy(f32[32,4096]{1,0:T(8,128)} %shard_map.127) | data formatting | bytes 1048576
